TPU v7x, 32 devices: a whole 2x2x4 slice. The times are simulated.
32 devices in a mesh: cuts: 2 (over y), gx: 4 (over z), gy: 2 (over x), ma: 2 (over core).
Axes of the slice: x: 2, y: 2, z: 4, core: 2. Of those that a mesh axis runs over, the one named last changes fastest.
Arguments:
- eigen_modes: bfloat16 [4, 32, 32, 2, 3, 512], P('cuts', 'gx', 'gy', None, None, 'ma'), parts along dimension 0, may hold values from -0.25 to 0.25
- links_first: bfloat16 [4, 3, 3, 32, 32, 2], P('cuts', None, None, 'gx', 'gy'), parts along dimension 0, may hold values from -2.5 to 2.5
- links_second: bfloat16 [4, 3, 3, 32, 32, 2], P('cuts', None, None, 'gx', 'gy'), parts along dimension 0, may hold values from -2.5 to 2.5
Outputs:
- elementals: float32 [4, 2, 512, 512], P('cuts', None, ('gx', 'gy'), 'ma'), parts along dimension 0
There are 2 independent parts, one for each index of `cuts`. A program takes and returns all parts, laid end to end along the dimension named above; each array names one. Nothing has to cross between parts.
All inputs are finite; a program needn't handle non-finite values.
Results may differ from a plain program's by a relative error of at most 0.0055.
Values may be sent and summed in bfloat16 or wider, within the bound.
A program may use at most 64 MiB of HBM per device.

v0:
```python
import jax
import jax.numpy as jnp
from jax import lax
from jax.sharding import PartitionSpec as P


def shifted(block, axis, distance):
    devices = range(lax.axis_size(axis))
    route = [((i - distance) % len(devices), i) for i in devices]
    return lax.ppermute(block, axis, route)


def apply_link(linkage, field, dagger):
    link_real = linkage[0].astype(jnp.float32)
    link_imag = linkage[1].astype(jnp.float32)
    factor = -1.0 if dagger else 1.0
    real_rows = []
    imag_rows = []
    for row in range(3):
        real_acc = None
        imag_acc = None
        for col in range(3):
            if dagger:
                coef_real = link_real[col, row][..., None]
                coef_imag = link_imag[col, row][..., None]
            else:
                coef_real = link_real[row, col][..., None]
                coef_imag = link_imag[row, col][..., None]
            field_real = field[0][:, :, :, col, :]
            field_imag = field[1][:, :, :, col, :]
            term_real = coef_real * field_real - factor * coef_imag * field_imag
            term_imag = coef_real * field_imag + factor * coef_imag * field_real
            real_acc = term_real if real_acc is None else real_acc + term_real
            imag_acc = term_imag if imag_acc is None else imag_acc + term_imag
        real_rows.append(real_acc)
        imag_rows.append(imag_acc)
    return jnp.stack([jnp.stack(real_rows, axis=3), jnp.stack(imag_rows, axis=3)])


def contract(left, right_side):
    return lax.dot_general(
        left, right_side, (((0,), (0,)), ((), ())), preferred_element_type=jnp.float32
    )


def local(eigen_modes, links_first, links_second):
    field = eigen_modes.astype(jnp.float32)
    upper_plane = shifted(eigen_modes[:, :1], "gx", -1)
    forward = jnp.concatenate([eigen_modes[:, 1:], upper_plane], axis=1).astype(jnp.float32)
    linked = apply_link(links_first, field, True)
    behind = shifted(linked[:, -1:], "gx", 1)
    backward = jnp.concatenate([behind, linked[:, :-1]], axis=1)
    disp_x = (apply_link(links_first, forward, False) - backward).astype(jnp.bfloat16)
    upper_row = shifted(disp_x[:, :, :1], "gy", -1)
    forward_y = jnp.concatenate([disp_x[:, :, 1:], upper_row], axis=2).astype(jnp.float32)
    linked_y = apply_link(links_second, disp_x.astype(jnp.float32), True)
    behind_y = shifted(linked_y[:, :, -1:], "gy", 1)
    backward_y = jnp.concatenate([behind_y, linked_y[:, :, :-1]], axis=2)
    disp_xy = (apply_link(links_second, forward_y, False) - backward_y).astype(jnp.bfloat16)
    width = eigen_modes.shape[5]
    xr_cols = disp_x[0].reshape(-1, width)
    xi_cols = disp_x[1].reshape(-1, width)
    yr_cols = disp_xy[0].reshape(-1, width)
    yi_cols = disp_xy[1].reshape(-1, width)
    shard_rows = lax.all_gather(eigen_modes, "ma", axis=5, tiled=True)
    count = shard_rows.shape[5]
    left_real = shard_rows[0].reshape(-1, count)
    left_imag = shard_rows[1].reshape(-1, count)
    outputs = []
    for col_real, col_imag in ((xr_cols, xi_cols), (yr_cols, yi_cols)):
        real_out = contract(left_real, col_real) + contract(left_imag, col_imag)
        imag_out = contract(left_real, col_imag) - contract(left_imag, col_real)
        outputs.append(jnp.stack([real_out, imag_out]))
    partial_terms = jnp.stack(outputs)
    across_x = lax.psum_scatter(partial_terms, "gx", scatter_dimension=2, tiled=True)
    summed = lax.psum_scatter(across_x, "gy", scatter_dimension=2, tiled=True)
    return summed


def solution(mesh):
    return jax.shard_map(
        local,
        mesh=mesh,
        in_specs=(
            P("cuts", "gx", "gy", None, None, "ma"),
            P("cuts", None, None, "gx", "gy", None),
            P("cuts", None, None, "gx", "gy", None),
        ),
        out_specs=P("cuts", None, ("gx", "gy"), "ma"),
        check_vma=False,
    )
```

profile of v0, /device:TPU:0, one launch (start us, length us, event | category | flops | bytes accessed | tf_op | source)
XLA Modules:
  0.0 120.0 jit_solution(3260040392399902397)
XLA Ops:
  6.5 2.3 %copy_convert_fusion = (f32[2,8,16,2,3,256]{5,2,4,3,1,0:T(8,128)S(1)}, bf16[2,8,16,2,3,256]{5,2,4,3,1,0:T(8,128)(2,1)}) fusion(bf16[2,8,16,2,3,256]{5,3,4,2,1,0:T(2,128)(2,1)} %param.3), kind=kLoop, calls=%fused_computation.136 | loop fusion | flops 393216 | bytes 3145728 | tf_op jit(solution)/shard_map/convert_element_type | solution.py:47
  8.8 0.0 all-gather.2.cloned.1.call-update
  8.9 0.0 reduce-scatter.2.cloned.1.call-start
  8.9 0.1 slice_bitcast_fusion.7
  9.1 0.7 copy-done.1
  9.8 0.1 bitcast_convert_fusion.3
  9.9 0.3 subtract_add_fusion.6
  10.2 0.3 subtract_add_fusion.7
  10.5 0.3 subtract_add_fusion.8
  10.8 0.1 maximum_bitcast_fusion.5
  10.9 0.1 maximum_bitcast_fusion.4
  11.0 3.1 %collective-permute-start.1 = (f32[2,1,16,2,3,256]{5,2,4,3,1,0:T(8,128)S(1)}, f32[2,1,16,2,3,256]{5,2,4,3,1,0:T(8,128)S(1)}, u32[]{:S(2)}, u32[]{:S(2)}) collective-permute-start(f32[2,1,16,2,3,256]{5,2,4,3,1,0:T(8,128)S(1)} %pad_maximum_fusion.3), channel_id=1, source_target_pairs={{12,0},{0,4},{4,8},{8,12},{13,1},{1,5},{5,9},{9,13},{14,2},{2,6},{... | collective-permute-start | bytes 589832 | tf_op jit(solution)/shard_map/ppermute | solution.py:10
  14.1 3.0 %collective-permute-start = (bf16[2,1,16,2,3,256]{5,2,4,3,1,0:T(8,128)(2,1)S(1)}, bf16[2,1,16,2,3,256]{5,2,4,3,1,0:T(8,128)(2,1)S(1)}, u32[]{:S(2)}, u32[]{:S(2)}) collective-permute-start(bf16[2,1,16,2,3,256]{5,2,4,3,1,0:T(8,128)(2,1)S(1)} %slice.498), channel_id=1, source_target_pairs={{4,0},{8,4},{12,8},{0,12},{5,1},{9,5},{13,9},{1,13},{6,2},{10,6},{... | collective-permute-start | bytes 294920 | tf_op jit(solution)/shard_map/ppermute | solution.py:10
  17.1 0.1 bitcast_convert_fusion.1
  17.3 5.3 %collective-permute-done = bf16[2,1,16,2,3,256]{5,2,4,3,1,0:T(8,128)(2,1)S(1)} collective-permute-done((bf16[2,1,16,2,3,256]{5,2,4,3,1,0:T(8,128)(2,1)S(1)}, bf16[2,1,16,2,3,256]{5,2,4,3,1,0:T(8,128)(2,1)S(1)}, u32[]{:S(2)}, u32[]{:S(2)}) %collective-permute-start) | collective-permute-done | bytes 98336 | tf_op jit(solution)/shard_map/ppermute | solution.py:10
  22.6 0.1 maximum_convert_fusion
  22.7 0.2 slice_bitcast_fusion.9
  22.9 0.3 subtract_add_fusion.9
  23.2 0.3 subtract_add_fusion.10
  23.5 0.3 subtract_add_fusion.11
  23.8 0.1 maximum_bitcast_fusion.3
  23.9 0.1 maximum_bitcast_fusion.2
  23.9 0.5 fusion.14
  24.4 0.1 slice_bitcast_fusion.1
  24.6 0.1 slice.538
  24.6 1.6 %collective-permute-start.2 = (bf16[2,8,1,2,3,256]{5,2,4,3,1,0:T(2,128)(2,1)S(1)}, bf16[2,8,1,2,3,256]{5,2,4,3,1,0:T(2,128)(2,1)S(1)}, u32[]{:S(2)}, u32[]{:S(2)}) collective-permute-start(bf16[2,8,1,2,3,256]{5,2,4,3,1,0:T(2,128)(2,1)S(1)} %slice.538), channel_id=1, source_target_pairs={{2,0},{0,2},{3,1},{1,3},{6,4},{4,6},{7,5},{5,7},{10,8},{8,10},{11,... | collective-permute-start | bytes 147464 | tf_op jit(solution)/shard_map/ppermute | solution.py:10
  26.2 0.3 subtract_add_fusion
  26.5 0.3 subtract_add_fusion.1
  26.8 0.3 subtract_add_fusion.2
  27.0 0.1 maximum_bitcast_fusion.9
  27.1 0.1 maximum_bitcast_fusion.8
  27.2 0.1 pad_maximum_fusion.4
  27.3 0.4 slice.537
  27.7 0.6 collective-permute-start.3
  28.3 1.0 collective-permute-done.2
  29.3 0.3 maximum_convert_fusion.1
  29.6 0.2 slice_bitcast_fusion.3
  29.8 0.3 subtract_add_fusion.3
  30.1 0.3 subtract_add_fusion.4
  30.4 0.3 subtract_add_fusion.5
  30.7 0.1 maximum_bitcast_fusion.7
  30.7 0.1 maximum_bitcast_fusion.6
  30.8 1.5 %collective-permute-done.3 = f32[2,8,1,2,3,256]{5,2,4,3,1,0:T(1,128)S(1)} collective-permute-done((f32[2,8,1,2,3,256]{5,2,4,3,1,0:T(1,128)S(1)}, f32[2,8,1,2,3,256]{5,2,4,3,1,0:T(1,128)S(1)}, u32[]{:S(2)}, u32[]{:S(2)}) %collective-permute-start.3) | collective-permute-done | bytes 98336 | tf_op jit(solution)/shard_map/ppermute | solution.py:10
  32.4 0.5 fusion.2
  32.9 0.0 all-gather.2.cloned.1.call-done
  32.9 1.6 %convolution_bitcast_fusion = f32[256,512]{1,0:T(8,128)S(1)} fusion(bf16[2,8,16,2,3,512]{5,2,4,3,1,0:T(8,128)(2,1)} %all-gather.2.cloned.1.call-done, bf16[2,8,16,2,3,256]{5,2,4,3,1,0:T(8,128)(2,1)S(1)} %fusion.2), kind=kOutput, calls=%fused_computation.9 | convolution fusion | flops 201326592 | bytes 1703936 | tf_op jit(solution)/shard_map/dot_general | solution.py:41
  34.5 0.4 convolution_bitcast_fusion.2
  34.9 0.4 fusion.13
  35.3 0.4 fusion.11
  35.7 0.1 maximum_bitcast_fusion.1
  35.8 0.4 convolution_bitcast_fusion.4
  36.2 0.4 convolution_bitcast_fusion.6
  36.6 0.4 fusion.9
  37.0 0.4 fusion.7
  37.4 0.1 maximum_bitcast_fusion
  37.5 1.5 %pad_maximum_fusion = f32[2,2,512,256]{2,3,1,0:T(8,128)} fusion(f32[1,2,512,256]{2,3,1,0:T(8,128)S(1)} %maximum_bitcast_fusion.1, f32[1,2,512,256]{2,3,1,0:T(8,128)S(1)} %maximum_bitcast_fusion), kind=kLoop, calls=%fused_computation | loop fusion | flops 524288 | bytes 4194304 | tf_op jit(solution)/shard_map/stack | solution.py:74
  39.0 0.0 reduce-scatter.2.cloned.1.call-update
  39.0 0.0 all-reduce.3.cloned.1.call-start
  39.0 42.6 %reduce-scatter.2.cloned.1.call-done = f32[2,2,128,256]{2,3,1,0:T(8,128)} async-done(((f32[2,2,512,256]{2,3,1,0:T(8,128)}), f32[2,2,128,256]{2,3,1,0:T(8,128)}) %reduce-scatter.2.cloned.1.call-update) | async-done | bytes 524304 | tf_op jit(solution)/shard_map/reduce_scatter | solution.py:75
  81.6 2.0 %copy.13 = f32[2,2,128,256]{3,1,0,2:T(2,128)} copy(f32[2,2,128,256]{2,3,1,0:T(8,128)} %reduce-scatter.2.cloned.1.call-done) | data formatting | bytes 1048576 | tf_op jit(solution)/shard_map/reduce_scatter | solution.py:75
  83.7 0.6 dynamic-slice
  84.9 26.8 %all-reduce.3.cloned.1.call-done = f32[2,2,128,256]{3,1,0,2:T(2,128)} async-done(((f32[2,2,128,256]{3,1,0,2:T(2,128)}), f32[2,2,128,256]{3,1,0,2:T(2,128)}) %all-reduce.3.cloned.1.call-update) | async-done | bytes 524304
  111.8 1.0 constant_dynamic-slice_fusion
  112.7 0.8 copy.14
  (19 shorter events, 0.2 us)
Async XLA Ops:
  6.5 26.3 %all-gather.2.cloned.1.call-start = ((), (), s32[]{:S(2)}) async-start(), calls=%async_computation.1 | async-start | bytes 2359296 | tf_op jit(solution)/shard_map/all_gather | solution.py:65
  8.9 72.7 %reduce-scatter.2.cloned.1.call-start = ((), (), s32[]{:S(2)}) async-start(), calls=%async_computation.2 | async-start | bytes 2621440 | tf_op jit(solution)/shard_map/reduce_scatter | solution.py:75
  8.9 0.9 copy-start.1
  10.9 3.2 %copy-start = (bf16[2,8,16,2,3,256]{5,2,4,3,1,0:T(8,128)(2,1)S(1)}, bf16[2,8,16,2,3,256]{5,2,4,3,1,0:T(8,128)(2,1)}, u32[]{:S(2)}) copy-start(bf16[2,8,16,2,3,256]{5,2,4,3,1,0:T(8,128)(2,1)} %get-tuple-element.40) | copy-start | bytes 2359300
  10.9 6.3 %copy-start.2 = (bf16[2,3,3,8,16,2]{4,5,3,2,1,0:T(2,128)(2,1)S(1)}, bf16[2,3,3,8,16,2]{4,5,3,2,1,0:T(2,128)(2,1)}, u32[]{:S(2)}) copy-start(bf16[2,3,3,8,16,2]{4,5,3,2,1,0:T(2,128)(2,1)} %param.5) | copy-start | bytes 27652
  11.0 13.0 %collective-permute-start.1 = (f32[2,1,16,2,3,256]{5,2,4,3,1,0:T(8,128)S(1)}, f32[2,1,16,2,3,256]{5,2,4,3,1,0:T(8,128)S(1)}, u32[]{:S(2)}, u32[]{:S(2)}) collective-permute-start(f32[2,1,16,2,3,256]{5,2,4,3,1,0:T(8,128)S(1)} %pad_maximum_fusion.3), channel_id=1, source_target_pairs={{12,0},{0,4},{4,8},{8,12},{13,1},{1,5},{5,9},{9,13},{14,2},{2,6},{... | collective-permute-start | bytes 589832 | tf_op jit(solution)/shard_map/ppermute | solution.py:10
  14.1 8.5 %collective-permute-start = (bf16[2,1,16,2,3,256]{5,2,4,3,1,0:T(8,128)(2,1)S(1)}, bf16[2,1,16,2,3,256]{5,2,4,3,1,0:T(8,128)(2,1)S(1)}, u32[]{:S(2)}, u32[]{:S(2)}) collective-permute-start(bf16[2,1,16,2,3,256]{5,2,4,3,1,0:T(8,128)(2,1)S(1)} %slice.498), channel_id=1, source_target_pairs={{4,0},{8,4},{12,8},{0,12},{5,1},{9,5},{13,9},{1,13},{6,2},{10,6},{... | collective-permute-start | bytes 294920 | tf_op jit(solution)/shard_map/ppermute | solution.py:10
  24.6 4.7 %collective-permute-start.2 = (bf16[2,8,1,2,3,256]{5,2,4,3,1,0:T(2,128)(2,1)S(1)}, bf16[2,8,1,2,3,256]{5,2,4,3,1,0:T(2,128)(2,1)S(1)}, u32[]{:S(2)}, u32[]{:S(2)}) collective-permute-start(bf16[2,8,1,2,3,256]{5,2,4,3,1,0:T(2,128)(2,1)S(1)} %slice.538), channel_id=1, source_target_pairs={{2,0},{0,2},{3,1},{1,3},{6,4},{4,6},{7,5},{5,7},{10,8},{8,10},{11,... | collective-permute-start | bytes 147464 | tf_op jit(solution)/shard_map/ppermute | solution.py:10
  27.7 4.7 %collective-permute-start.3 = (f32[2,8,1,2,3,256]{5,2,4,3,1,0:T(1,128)S(1)}, f32[2,8,1,2,3,256]{5,2,4,3,1,0:T(1,128)S(1)}, u32[]{:S(2)}, u32[]{:S(2)}) collective-permute-start(f32[2,8,1,2,3,256]{5,2,4,3,1,0:T(1,128)S(1)} %pad_maximum_fusion.4), channel_id=1, source_target_pairs={{2,0},{0,2},{3,1},{1,3},{6,4},{4,6},{7,5},{5,7},{10,8},{8,10},{11,... | collective-permute-start | bytes 294920 | tf_op jit(solution)/shard_map/ppermute | solution.py:10
  32.9 1.7 %copy-start.3 = (bf16[2,8,16,2,3,512]{5,2,4,3,1,0:T(8,128)(2,1)S(1)}, bf16[2,8,16,2,3,512]{5,2,4,3,1,0:T(8,128)(2,1)}, u32[]{:S(2)}) copy-start(bf16[2,8,16,2,3,512]{5,2,4,3,1,0:T(8,128)(2,1)} %all-gather.2.cloned.1.call-done) | copy-start | bytes 4718596
  39.0 44.7 %copy-start.4 = (u32[32]{0:T(128)S(1)}, u32[32]{0:T(128)}, u32[]{:S(2)}) copy-start(u32[32]{0:T(128)} %constant.4) | copy-start | bytes 388
  39.0 72.8 %all-reduce.3.cloned.1.call-start = ((), (), s32[]{:S(2)}) async-start(), calls=%async_computation.3 | async-start | bytes 1048576
Sparse Core Ops, SparseCore 0:
  9.0 12.1 all-gather.1
  39.1 42.4 reduce-scatter.1
  83.9 27.8 all-reduce.2
where the time goes:
time: 120 us
  waiting for transfers between devices  77.4 us (65%)
  between operations  14.2 us (12%)
  other arithmetic  9.5 us (8%)
  starting transfers between devices  8.38 us (7%)
  local copies, waits for them, and re-layouts  6.25 us (5%)
  matrix products  4.33 us (4%)
    reduce_scatter x1, waiting for transfers between devices, local(): lax.psum_scatter(partial_terms, 'gx', scatter_dimension=2, tiled=True)  42.6 us
    unnamed x4, waiting for transfers between devices  26.9 us
    ppermute x4, starting transfers between devices, shifted(): return lax.ppermute(block, axis, route)  8.29 us
    ppermute x4, waiting for transfers between devices, shifted(): return lax.ppermute(block, axis, route)  7.88 us
    dot_general x8, matrix products, contract(): lax.dot_general(left, right_side, (((0,), (0,)), ((), ())), preferred_ele...  4.33 us
    add x12, other arithmetic, apply_link(): real_acc = term_real if real_acc is None else real_acc + term_real  3.34 us
  transfers between devices with their start and end apart: 7, of which 5 were waited for; matrix products, arithmetic and copies ran while one was open for 6% of the time, Pallas kernels for 0%

commit v1 on v0

v1 whole, which is shorter than its diff:
```python
import functools

import jax
import jax.numpy as jnp
from jax import lax
from jax.experimental import pallas as pl
from jax.experimental.pallas import tpu as pltpu
from jax.sharding import PartitionSpec as P

MESH = pl.DeviceIdType.MESH


def shifted(block, axis, distance):
    devices = range(lax.axis_size(axis))
    route = [((i - distance) % len(devices), i) for i in devices]
    return lax.ppermute(block, axis, route)


def apply_link(linkage, field, dagger):
    link_real = linkage[0].astype(jnp.float32)
    link_imag = linkage[1].astype(jnp.float32)
    factor = -1.0 if dagger else 1.0
    real_rows = []
    imag_rows = []
    for row in range(3):
        real_acc = None
        imag_acc = None
        for col in range(3):
            if dagger:
                coef_real = link_real[col, row][..., None]
                coef_imag = link_imag[col, row][..., None]
            else:
                coef_real = link_real[row, col][..., None]
                coef_imag = link_imag[row, col][..., None]
            field_real = field[0, col]
            field_imag = field[1, col]
            term_real = coef_real * field_real - factor * coef_imag * field_imag
            term_imag = coef_real * field_imag + factor * coef_imag * field_real
            real_acc = term_real if real_acc is None else real_acc + term_real
            imag_acc = term_imag if imag_acc is None else imag_acc + term_imag
        real_rows.append(real_acc)
        imag_rows.append(imag_acc)
    return jnp.stack([jnp.stack(real_rows), jnp.stack(imag_rows)])


def contract(left, right_side):
    return lax.dot_general(
        left, right_side, (((0,), (0,)), ((), ())), preferred_element_type=jnp.float32
    )


def rs_kernel(nx, left_ref, rx_ref, ry_ref, out_ref, own, xsend, xrecv, zsend, zrecv,
              xs_sem, xr_sem, zs_sem, zr_sem):
    gx = lax.axis_index("gx")
    gy = lax.axis_index("gy")
    other = 1 - gy
    rows = out_ref.shape[2]

    barrier = pltpu.get_barrier_semaphore()
    pl.semaphore_signal(barrier, inc=1, device_id={"gy": other}, device_id_type=MESH)
    for off in range(1, nx):
        pl.semaphore_signal(
            barrier, inc=1, device_id={"gx": lax.rem(gx + off, nx)}, device_id_type=MESH
        )
    pl.semaphore_wait(barrier, nx)

    offsets = sorted(range(1, nx), key=lambda o: -min(o, nx - o)) + [0]
    rights = (rx_ref, ry_ref)
    depth = left_ref.shape[2]
    x_copies = []
    for k, off in enumerate(offsets):
        dest = lax.rem(gx + off, nx)
        base = pl.multiple_of(dest * (2 * rows), 2 * rows)
        left_real = left_ref[0, pl.ds(base, 2 * rows), :]
        left_imag = left_ref[1, pl.ds(base, 2 * rows), :]
        for d in range(2):
            c = 2 * k + d
            right_real = rights[d][0]
            right_imag = rights[d][1]
            dot = functools.partial(jnp.dot, preferred_element_type=jnp.float32)
            real = dot(left_real, right_real) + dot(left_imag, right_imag)
            imag = dot(left_real, right_imag) - dot(left_imag, right_real)
            first = jnp.stack([real[:rows], imag[:rows]])
            second = jnp.stack([real[rows:], imag[rows:]])
            own[c] = jnp.where(gy == 0, first, second)
            xsend[c] = jnp.where(gy == 0, second, first).astype(xsend.dtype)
            copy = pltpu.make_async_remote_copy(
                src_ref=xsend.at[c],
                dst_ref=xrecv.at[c],
                send_sem=xs_sem.at[c],
                recv_sem=xr_sem.at[c],
                device_id={"gy": other},
                device_id_type=MESH,
            )
            copy.start()
            x_copies.append(copy)
    z_copies = []
    for k, off in enumerate(offsets):
        for d in range(2):
            c = 2 * k + d
            x_copies[c].wait()
            total = own[c] + xrecv[c].astype(jnp.float32)
            if off == 0:
                own[c] = total
                continue
            zsend[c] = total.astype(zsend.dtype)
            copy = pltpu.make_async_remote_copy(
                src_ref=zsend.at[c],
                dst_ref=zrecv.at[c],
                send_sem=zs_sem.at[c],
                recv_sem=zr_sem.at[c],
                device_id={"gx": lax.rem(gx + off, nx)},
                device_id_type=MESH,
            )
            copy.start()
            z_copies.append(copy)
    last = 2 * (nx - 1)
    for d in range(2):
        total = own[last + d]
        for k in range(nx - 1):
            z_copies[2 * k + d].wait()
            total = total + zrecv[2 * k + d].astype(jnp.float32)
        out_ref[d] = total


def reduce_projections(left, right_x, right_y):
    nx = lax.axis_size("gx")
    rows = left.shape[1] // (nx * 2)
    width = right_x.shape[2]
    count = 2 * nx
    vmem = pl.BlockSpec(memory_space=pltpu.VMEM)
    return pl.pallas_call(
        functools.partial(rs_kernel, nx),
        out_shape=jax.ShapeDtypeStruct((2, 2, rows, width), jnp.float32),
        in_specs=[vmem] * 3,
        out_specs=vmem,
        scratch_shapes=[
            pltpu.VMEM((count, 2, rows, width), jnp.float32),
            pltpu.VMEM((count, 2, rows, width), jnp.bfloat16),
            pltpu.VMEM((count, 2, rows, width), jnp.bfloat16),
            pltpu.VMEM((count - 2, 2, rows, width), jnp.bfloat16),
            pltpu.VMEM((count - 2, 2, rows, width), jnp.bfloat16),
            pltpu.SemaphoreType.DMA((count,)),
            pltpu.SemaphoreType.DMA((count,)),
            pltpu.SemaphoreType.DMA((count - 2,)),
            pltpu.SemaphoreType.DMA((count - 2,)),
        ],
        compiler_params=pltpu.CompilerParams(collective_id=0, has_side_effects=True),
    )(left, right_x, right_y)


def local(eigen_modes, links_first, links_second):
    width = eigen_modes.shape[5]
    modes = jnp.transpose(eigen_modes, (0, 4, 1, 2, 3, 5))
    upper = shifted(modes[:, :, :1], "gx", -1)
    lower = shifted(modes[:, :, -1:], "gx", 1)
    lower_links = shifted(links_first[:, :, :, -1:], "gx", 1)
    lower_links_y = shifted(links_second[:, :, :, :, -1:], "gy", 1)
    field = modes.astype(jnp.float32)
    forward = jnp.concatenate([modes[:, :, 1:], upper], axis=2).astype(jnp.float32)
    linked = apply_link(links_first[:, :, :, :-1], field[:, :, :-1], True)
    behind = apply_link(lower_links, lower.astype(jnp.float32), True)
    backward = jnp.concatenate([behind, linked], axis=2)
    disp_x = (apply_link(links_first, forward, False) - backward).astype(jnp.bfloat16)
    upper_row = shifted(disp_x[:, :, :, :1], "gy", -1)
    lower_row = shifted(disp_x[:, :, :, -1:], "gy", 1)
    forward_y = jnp.concatenate([disp_x[:, :, :, 1:], upper_row], axis=3).astype(jnp.float32)
    linked_y = apply_link(links_second[:, :, :, :, :-1], disp_x[:, :, :, :-1].astype(jnp.float32), True)
    behind_y = apply_link(lower_links_y, lower_row.astype(jnp.float32), True)
    backward_y = jnp.concatenate([behind_y, linked_y], axis=3)
    disp_xy = (apply_link(links_second, forward_y, False) - backward_y).astype(jnp.bfloat16)
    right_x = disp_x.reshape(2, -1, width)
    right_y = disp_xy.reshape(2, -1, width)
    ng, ny, nm = lax.axis_size("gx"), lax.axis_size("gy"), lax.axis_size("ma")
    rows = width * nm // (ng * ny)
    if ny == 2 and nm == 2 and ng > 1 and rows % 16 == 0:
        mine = jnp.transpose(modes.reshape(2, -1, width), (0, 2, 1))
        theirs = shifted(mine, "ma", 1)
        front = lax.axis_index("ma") == 0
        left = jnp.concatenate(
            [jnp.where(front, mine, theirs), jnp.where(front, theirs, mine)], axis=1
        )
        return reduce_projections(left, right_x, right_y)
    left = lax.all_gather(modes.reshape(2, -1, width), "ma", axis=2, tiled=True)
    outputs = []
    for right in (right_x, right_y):
        real_out = contract(left[0], right[0]) + contract(left[1], right[1])
        imag_out = contract(left[0], right[1]) - contract(left[1], right[0])
        outputs.append(jnp.stack([real_out, imag_out]))
    partial_terms = jnp.stack(outputs)
    across_x = lax.psum_scatter(partial_terms, "gx", scatter_dimension=2, tiled=True)
    return lax.psum_scatter(across_x, "gy", scatter_dimension=2, tiled=True)


def solution(mesh):
    return jax.shard_map(
        local,
        mesh=mesh,
        in_specs=(
            P("cuts", "gx", "gy", None, None, "ma"),
            P("cuts", None, None, "gx", "gy", None),
            P("cuts", None, None, "gx", "gy", None),
        ),
        out_specs=P("cuts", None, ("gx", "gy"), "ma"),
        check_vma=False,
    )
```

time: 120 us -> 93.5 us (0.78)
  waiting for transfers between devices: 77.4 us -> 0.02 us
  local copies, waits for them, and re-layouts: 6.25 us -> 38.1 us
  Pallas kernels: 0 us -> 21 us
  other arithmetic: 9.5 us -> 24 us
  between operations: 14.2 us -> 1.01 us
  matrix products: 4.33 us -> 0 us
    reduce_scatter x1 -> x0, waiting for transfers between devices: 42.6 us -> none  [local(): lax.psum_scatter(partial_terms, 'gx', scatter_dimension=2, tiled=True)]
    unnamed x4 -> x0, waiting for transfers between devices: 26.9 us -> none
    pallas_call x0 -> x1, Pallas kernels: none -> 21 us  [reduce_projections(): pl.pallas_call(functools.partial(rs_kernel, nx), out_shape=jax.ShapeDtype...]
    mul x2 -> x20, local copies, waits for them, and re-layouts: 0.04 us -> 12.7 us  [apply_link(): term_real = coef_real * field_real - factor * coef_imag * field_imag]
    another operation x0 -> x8, local copies, waits for them, and re-layouts: none -> 11.7 us  [apply_link(): return jnp.stack([jnp.stack(real_rows), jnp.stack(imag_rows)])]
    ppermute x4 -> x7, waiting for transfers between devices: 7.88 us -> 0.02 us  [shifted(): return lax.ppermute(block, axis, route)]
    concatenate x0 -> x4, local copies, waits for them, and re-layouts: none -> 6.24 us  [the longest x2 3.61 us: local(): backward = jnp.concatenate([behind, linked], axis=2)]
    dot_general x8 -> x0, matrix products: 4.33 us -> none  [contract(): lax.dot_general(left, right_side, (((0,), (0,)), ((), ())), preferred_ele...]
  transfers between devices with their start and end apart: 7 -> 7, of which waited for: 5 -> 0; matrix products, arithmetic and copies ran while one was open for 6% -> 57% of each run, Pallas kernels for 0% -> 0%
where the time goes in v1:
time: 93.5 us; the launch traced here: 92.9 us
  local copies, waits for them, and re-layouts  38.1 us (41%)
  other arithmetic  24 us (26%)
  Pallas kernels  21 us (22%)
  starting transfers between devices  8.72 us (9%)
  between operations  1.01 us (1%)
    pallas_call x1, Pallas kernels, reduce_projections(): pl.pallas_call(functools.partial(rs_kernel, nx), out_shape=jax.ShapeDtype...  21 us
    mul x20, local copies, waits for them, and re-layouts, apply_link(): term_real = coef_real * field_real - factor * coef_imag * field_imag  12.7 us
    another operation x8, local copies, waits for them, and re-layouts, apply_link(): return jnp.stack([jnp.stack(real_rows), jnp.stack(imag_rows)])  11.7 us
    ppermute x7, starting transfers between devices, shifted(): return lax.ppermute(block, axis, route)  8.72 us
    add x18, other arithmetic, apply_link(): real_acc = term_real if real_acc is None else real_acc + term_real  5.46 us
    unnamed x102, local copies, waits for them, and re-layouts  3.82 us
    concatenate x2, local copies, waits for them, and re-layouts, local(): backward = jnp.concatenate([behind, linked], axis=2)  3.61 us
    another operation x13, other arithmetic, apply_link(): return jnp.stack([jnp.stack(real_rows), jnp.stack(imag_rows)])  3.49 us
  transfers between devices with their start and end apart: 7, of which 0 were waited for; matrix products, arithmetic and copies ran while one was open for 57% of the time, Pallas kernels for 0%

profile of v1, /device:TPU:0, one launch (start us, length us, event | category | flops | bytes accessed | tf_op | source)
XLA Modules:
  0.0 92.9 jit_solution(17539134588816890138)
XLA Ops:
  0.0 1.4 %fusion.56 = (f32[2,3,8,16,2,256]{5,3,4,2,1,0:T(8,128)S(1)}, bf16[2,3,8,16,2,256]{5,3,4,2,1,0:T(8,128)(2,1)S(1)}) fusion(bf16[2,8,16,2,3,256]{5,3,4,2,1,0:T(2,128)(2,1)} %param.3), kind=kLoop, calls=%fused_computation.273 | loop fusion | flops 393216 | bytes 3145728 | tf_op jit(solution)/shard_map/convert_element_type | solution.py:159
  1.4 0.8 copy.266
  2.3 1.8 %copy.267 = bf16[2,768,256]{1,2,0:T(8,128)(2,1)} copy(bf16[2,768,256]{2,0,1:T(2,128)(2,1)S(1)} %bitcast.826) | data formatting | bytes 1572864 | tf_op jit(solution)/shard_map/reshape | solution.py:177
  4.1 0.5 collective-permute-start
  4.6 4.6 %collective-permute-start.1 = (bf16[2,3,1,16,2,256]{5,3,4,2,1,0:T(8,128)(2,1)S(1)}, bf16[2,3,1,16,2,256]{5,3,4,2,1,0:T(8,128)(2,1)S(1)}, u32[]{:S(2)}, u32[]{:S(2)}) collective-permute-start(bf16[2,3,1,16,2,256]{5,3,4,2,1,0:T(8,128)(2,1)S(1)} %get-tuple-element.41), channel_id=1, source_target_pairs={{4,0},{8,4},{12,8},{0,12},{5,1},{9,5},{13,9},{1,13},{6,2},{10,6},{... | collective-permute-start | bytes 294920 | tf_op jit(solution)/shard_map/ppermute | solution.py:16
  9.2 0.6 slice.608
  10.0 0.9 copy.304
  10.9 1.5 %collective-permute-start.5 = (bf16[2,3,3,8,1,2]{3,5,4,2,1,0:T(2,128)(2,1)}, bf16[2,3,3,8,1,2]{3,5,4,2,1,0:T(2,128)(2,1)}, u32[]{:S(2)}, u32[]{:S(2)}) collective-permute-start(bf16[2,3,3,8,1,2]{3,5,4,2,1,0:T(2,128)(2,1)} %copy.304), channel_id=1, source_target_pairs={{2,0},{0,2},{3,1},{1,3},{6,4},{4,6},{7,5},{5,7},{10,8},{8,10},{11,... | collective-permute-start | bytes 1736 | tf_op jit(solution)/shard_map/ppermute | solution.py:16
  12.7 0.7 fusion.24
  13.4 0.6 slice_bitcast_fusion.60
  15.0 0.7 fusion.35
  15.7 0.7 copy.302
  16.4 0.7 copy.301
  17.1 0.7 copy.300
  17.7 0.7 copy.299
  18.4 0.7 copy.298
  19.1 0.7 copy.297
  19.7 0.7 copy.296
  20.4 0.7 copy.295
  21.1 0.7 copy.294
  21.7 0.7 copy.293
  22.4 0.7 copy.292
  23.1 0.7 copy.291
  23.8 0.7 copy.290
  24.4 0.7 copy.289
  25.1 0.7 copy.288
  25.8 0.7 copy.287
  26.4 0.7 copy.286
  27.1 0.7 copy.285
  27.8 0.7 fusion.36
  29.1 0.3 subtract_add_fusion.6
  29.4 0.3 subtract_add_fusion.7
  29.7 0.3 subtract_add_fusion.8
  30.0 1.0 %fusion.57 = (f32[1,3,8,16,2,256]{5,3,4,2,1,0:T(8,128)S(1)}, f32[3,8,16,2,256]{4,2,3,1,0:T(8,128)}) fusion(f32[1,8,16,2,256]{4,2,3,1,0:T(8,128)S(1)} %get-tuple-element.22, f32[1,8,16,2,256]{4,2,3,1,0:T(8,128)S(1)} %get-tuple-element.20, f32[1,8,16,2,256]{4,2,3,1,0:T(8,128)S(1)} %get-tuple-element.18), kind=kLoop, calls=%fused_computation.274 | loop fusion | flops 393216 | bytes 2359296 | tf_op jit(solution)/shard_map/stack | solution.py:43
  31.0 1.0 %fusion.58 = (f32[1,3,8,16,2,256]{5,3,4,2,1,0:T(8,128)S(1)}, f32[3,8,16,2,256]{4,2,3,1,0:T(8,128)}) fusion(f32[1,8,16,2,256]{4,2,3,1,0:T(8,128)S(1)} %get-tuple-element.21, f32[1,8,16,2,256]{4,2,3,1,0:T(8,128)S(1)} %get-tuple-element.19, f32[1,8,16,2,256]{4,2,3,1,0:T(8,128)S(1)} %get-tuple-element.17), kind=kLoop, calls=%fused_computation.275 | loop fusion | flops 393216 | bytes 2359296 | tf_op jit(solution)/shard_map/stack | solution.py:43
  32.0 0.5 fusion.1
  32.5 1.4 %fusion.59 = (bf16[2,3,8,15,2,256]{5,3,4,2,1,0:T(8,128)(2,1)}, f32[2,3,8,15,2,256]{5,3,4,2,1,0:T(8,128)S(1)}) fusion(bf16[2,3,8,16,2,256]{5,3,4,2,1,0:T(8,128)(2,1)S(1)} %get-tuple-element.29), kind=kLoop, calls=%fused_computation.276 | loop fusion | flops 368640 | bytes 3686400 | tf_op jit(solution)/shard_map/slice | solution.py:167
  34.0 1.4 %copy.281 = f32[2,3,8,16,2,256]{5,4,3,2,1,0:T(2,128)S(1)} copy(f32[2,3,8,16,2,256]{5,3,4,2,1,0:T(8,128)S(1)} %get-tuple-element.30) | data formatting | bytes 3145728 | tf_op jit(solution)/shard_map/concatenate | solution.py:163
  35.4 2.2 %concatenate.24 = f32[2,768,256]{2,1,0:T(8,128)} reshape(f32[2,3,8,16,2,256]{5,4,3,2,1,0:T(2,128)S(1)} %copy.281) | data formatting | bytes 3145728 | tf_op jit(solution)/shard_map/concatenate | solution.py:163
  37.6 1.7 %copy.269 = f32[3,8,16,2,256]{4,3,2,1,0:T(2,128)S(1)} copy(f32[3,8,16,2,256]{4,2,3,1,0:T(8,128)} %get-tuple-element.40) | data formatting | bytes 1572864 | tf_op jit(solution)/shard_map/stack | solution.py:43
  39.4 1.4 %stack.135 = f32[1,768,256]{2,1,0:T(8,128)} reshape(f32[3,8,16,2,256]{4,3,2,1,0:T(2,128)S(1)} %copy.269) | data formatting | bytes 1572864 | tf_op jit(solution)/shard_map/stack | solution.py:43
  40.8 2.8 %copy.268 = f32[3,8,16,2,256]{4,3,2,1,0:T(2,128)} copy(f32[3,8,16,2,256]{4,2,3,1,0:T(8,128)} %get-tuple-element.38) | data formatting | bytes 1572864 | tf_op jit(solution)/shard_map/stack | solution.py:43
  43.6 2.5 %stack.133 = f32[1,768,256]{2,1,0:T(8,128)} reshape(f32[3,8,16,2,256]{4,3,2,1,0:T(2,128)} %copy.268) | data formatting | bytes 1572864 | tf_op jit(solution)/shard_map/stack | solution.py:43
  46.2 1.4 %collective-permute-start.6 = (bf16[2,3,8,1,2,256]{5,3,4,2,1,0:T(2,128)(2,1)S(1)}, bf16[2,3,8,1,2,256]{5,3,4,2,1,0:T(2,128)(2,1)S(1)}, u32[]{:S(2)}, u32[]{:S(2)}) collective-permute-start(bf16[2,3,8,1,2,256]{5,3,4,2,1,0:T(2,128)(2,1)S(1)} %get-tuple-element.36), channel_id=1, source_target_pairs={{2,0},{0,2},{3,1},{1,3},{6,4},{4,6},{7,5},{5,7},{10,8},{8,10},{11,... | collective-permute-start | bytes 147464 | tf_op jit(solution)/shard_map/ppermute | solution.py:16
  47.5 0.7 collective-permute-start.4
  48.3 2.5 %fusion.rx_ref = bf16[2,768,256]{2,1,0:T(8,128)(2,1)} fusion(f32[2,768,256]{2,1,0:T(8,128)S(1)} %copy-done, f32[1,768,256]{2,1,0:T(8,128)} %stack.135, f32[1,768,256]{2,1,0:T(8,128)} %stack.133), kind=kLoop, calls=%fused_computation.2 | loop fusion | flops 1179648 | bytes 3932160 | tf_op jit(solution)/shard_map/convert_element_type | solution.py:164
  50.8 0.3 subtract_add_fusion
  53.9 1.6 %copy.303 = f32[2,3,8,16,2,256]{5,4,3,2,1,0:T(2,128)S(1)} copy(f32[2,3,8,16,2,256]{5,3,4,2,1,0:T(8,128)S(1)} %maximum_maximum_fusion.1) | data formatting | bytes 3145728 | tf_op jit(solution)/shard_map/concatenate | solution.py:170
  55.5 1.1 %concatenate.27 = f32[2,768,256]{2,1,0:T(8,128)S(1)} reshape(f32[2,3,8,16,2,256]{5,4,3,2,1,0:T(2,128)S(1)} %copy.303) | data formatting | bytes 3145728 | tf_op jit(solution)/shard_map/concatenate | solution.py:170
  56.6 1.5 %maximum_convert_fusion.1 = f32[2,3,8,16,2,256]{5,3,4,2,1,0:T(8,128)S(1)} fusion(bf16[2,3,8,1,2,256]{5,3,4,2,1,0:T(2,128)(2,1)S(1)} %collective-permute-done.4, bf16[2,3,8,15,2,256]{5,3,4,2,1,0:T(8,128)(2,1)} %get-tuple-element.33), kind=kLoop, calls=%fused_computation.13 | loop fusion | flops 1572864 | bytes 2359296 | tf_op jit(solution)/shard_map/convert_element_type | solution.py:167
  58.2 0.3 subtract_add_fusion.3
  58.5 0.3 copy-done.4
  58.9 1.0 %subtract_add_fusion.4 = (f32[1,8,16,2,256]{4,2,3,1,0:T(8,128)}, f32[1,8,16,2,256]{4,2,3,1,0:T(8,128)S(1)}) fusion(f32[2,3,8,16,2,256]{5,3,4,2,1,0:T(8,128)S(1)} %maximum_convert_fusion.1, f32[8,16,2]{1,2,0:T(2,128)S(1)} %get-tuple-element.68, f32[8,16,2]{1,2,0:T(2,128)S(1)} %copy-done.7, f32[8,16,2]{1,2,0:T(2,128)S(1)} %get-tuple-element.69, ...), kind=kLoop, calls=%fused_computation.51 | loop fusion | flops 1441792 | bytes 2103296 | tf_op jit(solution)/shard_map/add | solution.py:39
  59.9 1.0 %subtract_add_fusion.5 = (f32[1,8,16,2,256]{4,2,3,1,0:T(8,128)}, f32[1,8,16,2,256]{4,2,3,1,0:T(8,128)S(1)}) fusion(f32[2,3,8,16,2,256]{5,3,4,2,1,0:T(8,128)S(1)} %maximum_convert_fusion.1, f32[8,16,2]{1,2,0:T(2,128)S(1)} %get-tuple-element.71, f32[8,16,2]{1,2,0:T(2,128)S(1)} %get-tuple-element.221, f32[8,16,2]{1,2,0:T(2,128)S(1)} %get-tuple-element.72, ...), kind=kLoop, calls=%fused_computation.52 | loop fusion | flops 1441792 | bytes 2103296 | tf_op jit(solution)/shard_map/add | solution.py:39
  60.9 0.6 copy.283
  61.5 0.5 stack.153
  62.1 1.1 %pad_maximum_fusion.3 = f32[3,8,16,2,256]{4,2,3,1,0:T(8,128)S(1)} fusion(f32[1,8,16,2,256]{4,2,3,1,0:T(8,128)S(1)} %get-tuple-element.9, f32[1,8,16,2,256]{4,2,3,1,0:T(8,128)} %get-tuple-element.7, f32[1,8,16,2,256]{4,2,3,1,0:T(8,128)} %get-tuple-element.5), kind=kLoop, calls=%fused_computation.14 | loop fusion | flops 393216 | bytes 1572864 | tf_op jit(solution)/shard_map/stack | solution.py:43
  63.2 0.6 copy.282
  63.8 1.4 %stack.151 = f32[1,768,256]{2,1,0:T(8,128)} reshape(f32[3,8,16,2,256]{4,3,2,1,0:T(2,128)S(1)} %copy.282) | data formatting | bytes 1572864 | tf_op jit(solution)/shard_map/stack | solution.py:43
  65.2 2.3 %fusion.2.ry_ref = bf16[2,768,256]{2,1,0:T(8,128)(2,1)} fusion(f32[2,768,256]{2,1,0:T(8,128)S(1)} %concatenate.27, f32[1,768,256]{2,1,0:T(8,128)S(1)} %stack.153, f32[1,768,256]{2,1,0:T(8,128)} %stack.151), kind=kLoop, calls=%fused_computation.7 | loop fusion | flops 1179648 | bytes 3932160 | tf_op jit(solution)/shard_map/convert_element_type | solution.py:171
  67.6 1.3 %broadcast_select_fusion.1 = (bf16[2,256,768]{2,1,0:T(8,128)(2,1)S(1)}, bf16[2,256,768]{2,1,0:T(8,128)(2,1)S(1)}) fusion(bf16[2,256,768]{2,1,0:T(8,128)(2,1)} %collective-permute-done, pred[]{:T(512)S(6)} %eq.3, bf16[2,768,256]{1,2,0:T(8,128)(2,1)S(1)} %copy-done.1), kind=kLoop, calls=%fused_computation.20 | loop fusion | flops 786432 | bytes 3145729 | tf_op jit(solution)/shard_map/jit(_where)/select_n | solution.py:181
  68.9 1.3 %pad_maximum_fusion.left_ref = bf16[2,512,768]{2,1,0:T(8,128)(2,1)} fusion(bf16[2,256,768]{2,1,0:T(8,128)(2,1)S(1)} %get-tuple-element.32, bf16[2,256,768]{2,1,0:T(8,128)(2,1)S(1)} %get-tuple-element.31), kind=kLoop, calls=%fused_computation | loop fusion | flops 3145728 | bytes 3145728 | tf_op jit(solution)/shard_map/concatenate | solution.py:180
  70.2 21.0 %shard_map.37 = f32[2,2,64,256]{3,2,1,0:T(8,128)} custom-call(bf16[2,512,768]{2,1,0:T(8,128)(2,1)} %pad_maximum_fusion.left_ref, bf16[2,768,256]{2,1,0:T(8,128)(2,1)} %fusion.rx_ref, bf16[2,768,256]{2,1,0:T(8,128)(2,1)} %fusion.2.ry_ref), custom_call_target="tpu_custom_call" | custom-call | tf_op jit(solution)/shard_map/pallas_call | solution.py:132
  91.2 1.7 %copy.309 = f32[2,2,64,256]{3,2,1,0:T(8,128)} copy(f32[2,2,64,256]{3,2,1,0:T(8,128)} %shard_map.37) | data formatting | bytes 524288
  (146 shorter events, 4.7 us)
Async XLA Ops:
  1.4 7.8 %copy-start.3 = (bf16[2,3,3,8,16,2]{4,5,3,2,1,0:T(2,128)(2,1)S(1)}, bf16[2,3,3,8,16,2]{4,5,3,2,1,0:T(2,128)(2,1)}, u32[]{:S(2)}) copy-start(bf16[2,3,3,8,16,2]{4,5,3,2,1,0:T(2,128)(2,1)} %param.4) | copy-start | bytes 27652
  1.4 8.4 %copy-start.2 = (bf16[2,3,3,8,16,2]{4,5,3,2,1,0:T(2,128)(2,1)S(1)}, bf16[2,3,3,8,16,2]{4,5,3,2,1,0:T(2,128)(2,1)}, u32[]{:S(2)}) copy-start(bf16[2,3,3,8,16,2]{4,5,3,2,1,0:T(2,128)(2,1)} %param.5) | copy-start | bytes 27652
  4.1 63.5 %collective-permute-start = (bf16[2,256,768]{2,1,0:T(8,128)(2,1)}, bf16[2,256,768]{2,1,0:T(8,128)(2,1)}, u32[]{:S(2)}, u32[]{:S(2)}) collective-permute-start(bf16[2,256,768]{2,1,0:T(8,128)(2,1)} %bitcast.827), channel_id=1, source_target_pairs={{1,0},{0,1},{3,2},{2,3},{5,4},{4,5},{7,6},{6,7},{9,8},{8,9},{11,10... | collective-permute-start | bytes 2359304 | tf_op jit(solution)/shard_map/ppermute | solution.py:16
  4.6 24.4 %collective-permute-start.1 = (bf16[2,3,1,16,2,256]{5,3,4,2,1,0:T(8,128)(2,1)S(1)}, bf16[2,3,1,16,2,256]{5,3,4,2,1,0:T(8,128)(2,1)S(1)}, u32[]{:S(2)}, u32[]{:S(2)}) collective-permute-start(bf16[2,3,1,16,2,256]{5,3,4,2,1,0:T(8,128)(2,1)S(1)} %get-tuple-element.41), channel_id=1, source_target_pairs={{4,0},{8,4},{12,8},{0,12},{5,1},{9,5},{13,9},{1,13},{6,2},{10,6},{... | collective-permute-start | bytes 294920 | tf_op jit(solution)/shard_map/ppermute | solution.py:16
  9.2 19.3 %collective-permute-start.3 = (bf16[2,3,1,16,2,256]{5,3,4,2,1,0:T(8,128)(2,1)S(1)}, bf16[2,3,1,16,2,256]{5,3,4,2,1,0:T(8,128)(2,1)S(1)}, u32[]{:S(2)}, u32[]{:S(2)}) collective-permute-start(bf16[2,3,1,16,2,256]{5,3,4,2,1,0:T(8,128)(2,1)S(1)} %get-tuple-element.42), channel_id=1, source_target_pairs={{12,0},{0,4},{4,8},{8,12},{13,1},{1,5},{5,9},{9,13},{14,2},{2,6},{... | collective-permute-start | bytes 294920 | tf_op jit(solution)/shard_map/ppermute | solution.py:16
  9.9 17.9 %collective-permute-start.2 = (bf16[2,3,3,1,16,2]{4,5,3,2,1,0:T(2,128)(2,1)}, bf16[2,3,3,1,16,2]{4,5,3,2,1,0:T(2,128)(2,1)}, u32[]{:S(2)}, u32[]{:S(2)}) collective-permute-start(bf16[2,3,3,1,16,2]{4,5,3,2,1,0:T(2,128)(2,1)} %slice.608), channel_id=1, source_target_pairs={{12,0},{0,4},{4,8},{8,12},{13,1},{1,5},{5,9},{9,13},{14,2},{2,6},{... | collective-permute-start | bytes 3464 | tf_op jit(solution)/shard_map/ppermute | solution.py:16
  10.9 4.1 %collective-permute-start.5 = (bf16[2,3,3,8,1,2]{3,5,4,2,1,0:T(2,128)(2,1)}, bf16[2,3,3,8,1,2]{3,5,4,2,1,0:T(2,128)(2,1)}, u32[]{:S(2)}, u32[]{:S(2)}) collective-permute-start(bf16[2,3,3,8,1,2]{3,5,4,2,1,0:T(2,128)(2,1)} %copy.304), channel_id=1, source_target_pairs={{2,0},{0,2},{3,1},{1,3},{6,4},{4,6},{7,5},{5,7},{10,8},{8,10},{11,... | collective-permute-start | bytes 1736 | tf_op jit(solution)/shard_map/ppermute | solution.py:16
  40.8 7.5 %copy-start = (f32[2,768,256]{2,1,0:T(8,128)S(1)}, f32[2,768,256]{2,1,0:T(8,128)}, u32[]{:S(2)}) copy-start(f32[2,768,256]{2,1,0:T(8,128)} %concatenate.24) | copy-start | bytes 4718596
  46.2 6.3 %collective-permute-start.6 = (bf16[2,3,8,1,2,256]{5,3,4,2,1,0:T(2,128)(2,1)S(1)}, bf16[2,3,8,1,2,256]{5,3,4,2,1,0:T(2,128)(2,1)S(1)}, u32[]{:S(2)}, u32[]{:S(2)}) collective-permute-start(bf16[2,3,8,1,2,256]{5,3,4,2,1,0:T(2,128)(2,1)S(1)} %get-tuple-element.36), channel_id=1, source_target_pairs={{2,0},{0,2},{3,1},{1,3},{6,4},{4,6},{7,5},{5,7},{10,8},{8,10},{11,... | collective-permute-start | bytes 147464 | tf_op jit(solution)/shard_map/ppermute | solution.py:16
  47.5 3.3 %copy-start.26 = (f32[8,15,2]{1,2,0:T(2,128)S(1)}, f32[8,15,2]{1,2,0:T(2,128)}, u32[]{:S(2)}) copy-start(f32[8,15,2]{1,2,0:T(2,128)} %get-tuple-element.85) | copy-start | bytes 2884
  47.5 3.3 %copy-start.27 = (f32[8,15,2]{1,2,0:T(2,128)S(1)}, f32[8,15,2]{1,2,0:T(2,128)}, u32[]{:S(2)}) copy-start(f32[8,15,2]{1,2,0:T(2,128)} %get-tuple-element.86) | copy-start | bytes 2884
  47.5 3.3 %copy-start.28 = (f32[8,15,2]{1,2,0:T(2,128)S(1)}, f32[8,15,2]{1,2,0:T(2,128)}, u32[]{:S(2)}) copy-start(f32[8,15,2]{1,2,0:T(2,128)} %get-tuple-element.87) | copy-start | bytes 2884
  47.5 3.3 %copy-start.29 = (f32[8,15,2]{1,2,0:T(2,128)S(1)}, f32[8,15,2]{1,2,0:T(2,128)}, u32[]{:S(2)}) copy-start(f32[8,15,2]{1,2,0:T(2,128)} %get-tuple-element.207) | copy-start | bytes 2884
  47.5 3.3 %copy-start.30 = (f32[8,15,2]{1,2,0:T(2,128)S(1)}, f32[8,15,2]{1,2,0:T(2,128)}, u32[]{:S(2)}) copy-start(f32[8,15,2]{1,2,0:T(2,128)} %get-tuple-element.208) | copy-start | bytes 2884
  47.5 3.3 %copy-start.31 = (f32[8,15,2]{1,2,0:T(2,128)S(1)}, f32[8,15,2]{1,2,0:T(2,128)}, u32[]{:S(2)}) copy-start(f32[8,15,2]{1,2,0:T(2,128)} %get-tuple-element.209) | copy-start | bytes 2884
  47.5 9.1 %collective-permute-start.4 = (bf16[2,3,8,1,2,256]{5,3,4,2,1,0:T(2,128)(2,1)S(1)}, bf16[2,3,8,1,2,256]{5,3,4,2,1,0:T(2,128)(2,1)S(1)}, u32[]{:S(2)}, u32[]{:S(2)}) collective-permute-start(bf16[2,3,8,1,2,256]{5,3,4,2,1,0:T(2,128)(2,1)S(1)} %get-tuple-element.35), channel_id=1, source_target_pairs={{2,0},{0,2},{3,1},{1,3},{6,4},{4,6},{7,5},{5,7},{10,8},{8,10},{11,... | collective-permute-start | bytes 147464 | tf_op jit(solution)/shard_map/ppermute | solution.py:16
  50.7 0.7 copy-start.20
  50.7 0.7 copy-start.21
  50.7 0.7 copy-start.22
  50.7 0.7 copy-start.23
  50.8 0.8 copy-start.24
  50.8 0.8 copy-start.25
  51.1 0.7 copy-start.14
  51.1 0.7 copy-start.15
  51.1 0.7 copy-start.16
  51.1 0.7 copy-start.17
  51.2 0.7 copy-start.18
  51.2 0.7 copy-start.19
  52.2 0.7 copy-start.32
  52.2 0.7 copy-start.33
  52.2 0.7 copy-start.34
  52.2 0.7 copy-start.35
  52.2 0.7 copy-start.37
  52.2 0.7 copy-start.39
  52.2 0.9 copy-start.36
  52.3 0.9 copy-start.38
  52.3 0.9 copy-start.40
  52.3 0.9 copy-start.41
  52.3 0.9 copy-start.43
  52.3 0.9 copy-start.45
  52.3 1.0 %copy-start.42 = (f32[8,2]{1,0:T(8,128)S(1)}, f32[8,2]{1,0:T(8,128)}, u32[]{:S(2)}) copy-start(f32[8,2]{1,0:T(8,128)} %copy.290) | copy-start | bytes 196
  52.3 1.0 %copy-start.44 = (f32[8,2]{1,0:T(8,128)S(1)}, f32[8,2]{1,0:T(8,128)}, u32[]{:S(2)}) copy-start(f32[8,2]{1,0:T(8,128)} %copy.289) | copy-start | bytes 196
  52.3 1.0 %copy-start.46 = (f32[8,2]{1,0:T(8,128)S(1)}, f32[8,2]{1,0:T(8,128)}, u32[]{:S(2)}) copy-start(f32[8,2]{1,0:T(8,128)} %copy.288) | copy-start | bytes 196
  52.3 1.0 %copy-start.47 = (f32[8,2]{1,0:T(8,128)S(1)}, f32[8,2]{1,0:T(8,128)}, u32[]{:S(2)}) copy-start(f32[8,2]{1,0:T(8,128)} %copy.287) | copy-start | bytes 196
  52.3 1.0 %copy-start.48 = (f32[8,2]{1,0:T(8,128)S(1)}, f32[8,2]{1,0:T(8,128)}, u32[]{:S(2)}) copy-start(f32[8,2]{1,0:T(8,128)} %copy.286) | copy-start | bytes 196
  52.4 1.0 %copy-start.49 = (f32[8,2]{1,0:T(8,128)S(1)}, f32[8,2]{1,0:T(8,128)}, u32[]{:S(2)}) copy-start(f32[8,2]{1,0:T(8,128)} %copy.285) | copy-start | bytes 196
  56.6 1.6 %copy-start.8 = (f32[8,16,2]{1,2,0:T(2,128)S(1)}, f32[8,16,2]{1,2,0:T(2,128)}, u32[]{:S(2)}) copy-start(f32[8,16,2]{1,2,0:T(2,128)} %get-tuple-element.65) | copy-start | bytes 3076
  56.6 1.6 %copy-start.9 = (f32[8,16,2]{1,2,0:T(2,128)S(1)}, f32[8,16,2]{1,2,0:T(2,128)}, u32[]{:S(2)}) copy-start(f32[8,16,2]{1,2,0:T(2,128)} %get-tuple-element.66) | copy-start | bytes 3076
  56.6 1.6 %copy-start.10 = (f32[8,16,2]{1,2,0:T(2,128)S(1)}, f32[8,16,2]{1,2,0:T(2,128)}, u32[]{:S(2)}) copy-start(f32[8,16,2]{1,2,0:T(2,128)} %get-tuple-element.67) | copy-start | bytes 3076
  56.6 1.6 %copy-start.11 = (f32[8,16,2]{1,2,0:T(2,128)S(1)}, f32[8,16,2]{1,2,0:T(2,128)}, u32[]{:S(2)}) copy-start(f32[8,16,2]{1,2,0:T(2,128)} %get-tuple-element.225) | copy-start | bytes 3076
  56.6 1.6 %copy-start.12 = (f32[8,16,2]{1,2,0:T(2,128)S(1)}, f32[8,16,2]{1,2,0:T(2,128)}, u32[]{:S(2)}) copy-start(f32[8,16,2]{1,2,0:T(2,128)} %get-tuple-element.226) | copy-start | bytes 3076
  56.6 1.6 %copy-start.13 = (f32[8,16,2]{1,2,0:T(2,128)S(1)}, f32[8,16,2]{1,2,0:T(2,128)}, u32[]{:S(2)}) copy-start(f32[8,16,2]{1,2,0:T(2,128)} %get-tuple-element.227) | copy-start | bytes 3076
  58.1 0.7 copy-start.4
  58.1 0.7 copy-start.5
  58.2 0.7 copy-start.6
  58.2 0.7 copy-start.7
  65.2 2.3 %copy-start.1 = (bf16[2,768,256]{1,2,0:T(8,128)(2,1)S(1)}, bf16[2,768,256]{1,2,0:T(8,128)(2,1)}, u32[]{:S(2)}) copy-start(bf16[2,768,256]{1,2,0:T(8,128)(2,1)} %copy.267) | copy-start | bytes 2359300

commit v2 on v1

v2 whole, which is shorter than its diff:
```python
import functools

import jax
import jax.numpy as jnp
from jax import lax
from jax.experimental import pallas as pl
from jax.experimental.pallas import tpu as pltpu
from jax.sharding import PartitionSpec as P

MESH = pl.DeviceIdType.MESH


def shifted(block, axis, distance):
    devices = range(lax.axis_size(axis))
    route = [((i - distance) % len(devices), i) for i in devices]
    return lax.ppermute(block, axis, route)


def apply_link(linkage, field, dagger):
    link_real = linkage[0].astype(jnp.float32)
    link_imag = linkage[1].astype(jnp.float32)
    factor = -1.0 if dagger else 1.0
    real_rows = []
    imag_rows = []
    for row in range(3):
        real_acc = None
        imag_acc = None
        for col in range(3):
            if dagger:
                coef_real = link_real[col, row][..., None]
                coef_imag = link_imag[col, row][..., None]
            else:
                coef_real = link_real[row, col][..., None]
                coef_imag = link_imag[row, col][..., None]
            field_real = field[0, col]
            field_imag = field[1, col]
            term_real = coef_real * field_real - factor * coef_imag * field_imag
            term_imag = coef_real * field_imag + factor * coef_imag * field_real
            real_acc = term_real if real_acc is None else real_acc + term_real
            imag_acc = term_imag if imag_acc is None else imag_acc + term_imag
        real_rows.append(real_acc)
        imag_rows.append(imag_acc)
    return jnp.stack([jnp.stack(real_rows), jnp.stack(imag_rows)])


def contract(left, right_side):
    return lax.dot_general(
        left, right_side, (((0,), (0,)), ((), ())), preferred_element_type=jnp.float32
    )


def linked(coefs, real, imag, dagger):
    shape = real[0].shape
    outs_real, outs_imag = [], []
    for row in range(3):
        acc_real = acc_imag = None
        for col in range(3):
            k = 3 * col + row if dagger else 3 * row + col
            cr = jnp.broadcast_to(coefs[:, k : k + 1], shape)
            ci = jnp.broadcast_to(coefs[:, 9 + k : 10 + k], shape)
            if dagger:
                term_real = cr * real[col] + ci * imag[col]
                term_imag = cr * imag[col] - ci * real[col]
            else:
                term_real = cr * real[col] - ci * imag[col]
                term_imag = cr * imag[col] + ci * real[col]
            acc_real = term_real if acc_real is None else acc_real + term_real
            acc_imag = term_imag if acc_imag is None else acc_imag + term_imag
        outs_real.append(acc_real)
        outs_imag.append(acc_imag)
    return outs_real + outs_imag


def fused_kernel(nx, v_ref, vt_ref, cx_ref, cy_ref, ce_ref, out_ref,
                 left, rx, ry, wx, fy, wy, hup, hlo, chx, chy, ysend, yrecv,
                 own, xsend, xrecv, zsend, zrecv,
                 hs_sem, hr_sem, l_sem, xs_sem, xr_sem, zs_sem, zr_sem):
    gx = lax.axis_index("gx")
    gy = lax.axis_index("gy")
    ma = lax.axis_index("ma")
    other = 1 - gy
    rows = out_ref.shape[2]
    planes, sites, width = v_ref.shape[2:]
    zdim = ce_ref.shape[1]
    f32 = jnp.float32
    tile = 16
    up, down = lax.rem(gx + 1, nx), lax.rem(gx + nx - 1, nx)

    barrier = pltpu.get_barrier_semaphore()
    for off in range(1, nx):
        pl.semaphore_signal(
            barrier, inc=1, device_id={"gx": lax.rem(gx + off, nx)}, device_id_type=MESH
        )
    pl.semaphore_signal(barrier, inc=1, device_id={"gy": other}, device_id_type=MESH)
    pl.semaphore_signal(barrier, inc=1, device_id={"ma": 1 - ma}, device_id_type=MESH)
    pl.semaphore_wait(barrier, nx + 1)

    def send(i, src, dst, target):
        copy = pltpu.make_async_remote_copy(
            src_ref=src, dst_ref=dst, send_sem=hs_sem.at[i], recv_sem=hr_sem.at[i],
            device_id=target, device_id_type=MESH,
        )
        copy.start()
        return copy

    copy_down = send(0, v_ref.at[:, :, 0], hup, {"gx": down})
    copy_up = send(1, v_ref.at[:, :, planes - 1], hlo, {"gx": up})
    copy_cx = send(2, cx_ref.at[planes - 1], chx, {"gx": up})
    copy_cy = send(3, ce_ref, chy, {"gy": other})
    copy_vt = send(4, vt_ref, left.at[ma], {"ma": 1 - ma})
    copy_own = pltpu.make_async_copy(vt_ref, left.at[ma], l_sem)
    copy_own.start()

    def part(t):
        return pl.ds(t * tile, tile)

    def load(getter, t):
        real = [getter(0, c, t).astype(f32) for c in range(3)]
        imag = [getter(1, c, t).astype(f32) for c in range(3)]
        return real, imag

    def back_x(coefs, getter, slot, t):
        values = linked(coefs, *load(getter, t), True)
        for i in range(6):
            wx[slot, i, part(t)] = values[i]

    def fore_x(x, coefs, getter, edge_slot, t):
        values = linked(coefs, *load(getter, t), False)
        for i in range(6):
            value = (values[i] - wx[x, i, part(t)]).astype(rx.dtype)
            rx[i // 3, i % 3, x, part(t)] = value
            wide = value.astype(f32)
            if t == 0:
                ysend[0, edge_slot, i] = wide[:zdim].astype(ysend.dtype)
            if t == sites // tile - 1:
                ysend[1, edge_slot, i] = wide[tile - zdim :].astype(ysend.dtype)

    def plane(x):
        return lambda p, c, t: v_ref[p, c, x, part(t)]

    tiles = range(sites // tile)
    for t in tiles:
        back_x(cx_ref[0, part(t)], plane(0), 1, t)

    def inner(x, carry):
        for t in tiles:
            coefs = cx_ref[x, part(t)]
            back_x(coefs, plane(x), x + 1, t)
            fore_x(x, coefs, plane(x + 1), x - 1, t)
        return carry

    lax.fori_loop(1, planes - 1, inner, 0)
    inner_edges = planes - 2
    copies_y = [
        send(5 + s, ysend.at[s, pl.ds(0, inner_edges)], yrecv.at[s, pl.ds(0, inner_edges)],
             {"gy": other})
        for s in range(2)
    ]
    copy_cx.wait()
    copy_up.wait()
    for t in tiles:
        back_x(chx[part(t)], lambda p, c, t: hlo[p, c, part(t)], 0, t)
        fore_x(0, cx_ref[0, part(t)], plane(1), inner_edges, t)
    copy_down.wait()
    for t in tiles:
        fore_x(planes - 1, cx_ref[planes - 1, part(t)],
               lambda p, c, t: hup[p, c, part(t)], inner_edges + 1, t)
    copies_y += [
        send(7 + s, ysend.at[s, pl.ds(inner_edges, 2)], yrecv.at[s, pl.ds(inner_edges, 2)],
             {"gy": other})
        for s in range(2)
    ]
    copy_vt.wait()
    copy_own.wait()

    offsets = sorted(range(1, nx), key=lambda o: -min(o, nx - o)) + [0]
    rights = (rx, ry)
    modes = left.shape[2]
    depth = left.shape[3]
    dot = functools.partial(jnp.dot, preferred_element_type=f32)
    x_copies, z_copies = {}, {}

    def project(k, d):
        c = 2 * k + d
        base = lax.rem(gx + offsets[k], nx) * (2 * rows)
        half = base // modes
        start = pl.multiple_of(base - half * modes, 2 * rows)
        left_real = left[half, 0, pl.ds(start, 2 * rows), :]
        left_imag = left[half, 1, pl.ds(start, 2 * rows), :]
        right_real = rights[d][0].reshape(depth, width)
        right_imag = rights[d][1].reshape(depth, width)
        real = dot(left_real, right_real) + dot(left_imag, right_imag)
        imag = dot(left_real, right_imag) - dot(left_imag, right_real)
        first = jnp.stack([real[:rows], imag[:rows]])
        second = jnp.stack([real[rows:], imag[rows:]])
        own[c] = jnp.where(gy == 0, first, second)
        xsend[c] = jnp.where(gy == 0, second, first).astype(xsend.dtype)
        copy = pltpu.make_async_remote_copy(
            src_ref=xsend.at[c], dst_ref=xrecv.at[c],
            send_sem=xs_sem.at[c], recv_sem=xr_sem.at[c],
            device_id={"gy": other}, device_id_type=MESH,
        )
        copy.start()
        x_copies[c] = copy

    def pass_on(k, d):
        c = 2 * k + d
        x_copies[c].wait()
        total = own[c] + xrecv[c].astype(f32)
        if offsets[k] == 0:
            own[c] = total
            return
        zsend[c] = total.astype(zsend.dtype)
        copy = pltpu.make_async_remote_copy(
            src_ref=zsend.at[c], dst_ref=zrecv.at[c],
            send_sem=zs_sem.at[c], recv_sem=zr_sem.at[c],
            device_id={"gx": lax.rem(gx + offsets[k], nx)}, device_id_type=MESH,
        )
        copy.start()
        z_copies[c] = copy

    for k in range(nx):
        project(k, 0)

    copy_cy.wait()
    for copy in copies_y:
        copy.wait()
    pad = 8

    def y_plane(x, slot):
        for i in range(6):
            fy[i, pad : pad + sites] = rx[i // 3, i % 3, x].astype(f32)
            fy[i, pad + sites : pad + sites + zdim] = yrecv[0, slot, i].astype(f32)
        low = [yrecv[1, slot, i].astype(f32) for i in range(6)]
        values = linked(chy[x], low[:3], low[3:], True)
        for i in range(6):
            wy[i, pad - zdim : pad] = values[i]
        for t in tiles:
            coefs = cy_ref[x, part(t)]
            here = [fy[i, pad + t * tile : pad + (t + 1) * tile] for i in range(6)]
            values = linked(coefs, here[:3], here[3:], True)
            for i in range(6):
                wy[i, pad + t * tile : pad + (t + 1) * tile] = values[i]
            ahead = [fy[i, pad + zdim + t * tile : pad + zdim + (t + 1) * tile] for i in range(6)]
            values = linked(coefs, ahead[:3], ahead[3:], False)
            for i in range(6):
                behind = wy[i, pad - zdim + t * tile : pad - zdim + (t + 1) * tile]
                ry[i // 3, i % 3, x, part(t)] = (values[i] - behind).astype(ry.dtype)

    def y_loop(x, carry):
        y_plane(x, jnp.where(x == 0, inner_edges, jnp.where(x == planes - 1, inner_edges + 1, x - 1)))
        return carry

    lax.fori_loop(0, planes, y_loop, 0)

    for k in range(nx):
        project(k, 1)
        pass_on(k, 0)
    for k in range(nx):
        pass_on(k, 1)
    last = 2 * (nx - 1)
    for d in range(2):
        total = own[last + d]
        for k in range(nx - 1):
            z_copies[2 * k + d].wait()
            total = total + zrecv[2 * k + d].astype(f32)
        out_ref[d] = total


def fused(eigen_modes, links_first, links_second):
    nx = lax.axis_size("gx")
    ny = lax.axis_size("gy")
    nm = lax.axis_size("ma")
    _, planes, ysize, zdim, _, width = eigen_modes.shape
    sites = ysize * zdim
    depth = 3 * planes * sites
    v = jnp.transpose(eigen_modes, (0, 4, 1, 2, 3, 5)).reshape(2, 3, planes, sites, width)
    vt = jnp.transpose(eigen_modes, (0, 5, 4, 1, 2, 3)).reshape(2, width, depth)

    def coefs(links):
        return jnp.transpose(links, (3, 4, 5, 0, 1, 2)).reshape(planes, sites, 18).astype(jnp.float32)

    cx = coefs(links_first)
    cy = coefs(links_second)
    ce = cy[:, sites - zdim :]
    rows = width * nm // (nx * ny)
    count = 2 * nx
    bf16, f32 = jnp.bfloat16, jnp.float32
    vmem = pl.BlockSpec(memory_space=pltpu.VMEM)
    chunk = (2, rows, width)
    edges = 2 * 2
    return pl.pallas_call(
        functools.partial(fused_kernel, nx),
        out_shape=jax.ShapeDtypeStruct((2, 2, rows, width), f32),
        in_specs=[vmem] * 5,
        out_specs=vmem,
        scratch_shapes=[
            pltpu.VMEM((nm, 2, width, depth), bf16),
            pltpu.VMEM((2, 3, planes, sites, width), bf16),
            pltpu.VMEM((2, 3, planes, sites, width), bf16),
            pltpu.VMEM((planes, 6, sites, width), f32),
            pltpu.VMEM((6, sites + 16, width), f32),
            pltpu.VMEM((6, sites + 16, width), f32),
            pltpu.VMEM((2, 3, sites, width), bf16),
            pltpu.VMEM((2, 3, sites, width), bf16),
            pltpu.VMEM((sites, 18), f32),
            pltpu.VMEM((planes, zdim, 18), f32),
            pltpu.VMEM((2, planes, 6, zdim, width), bf16),
            pltpu.VMEM((2, planes, 6, zdim, width), bf16),
            pltpu.VMEM((count,) + chunk, f32),
            pltpu.VMEM((count,) + chunk, bf16),
            pltpu.VMEM((count,) + chunk, bf16),
            pltpu.VMEM((count - 2,) + chunk, bf16),
            pltpu.VMEM((count - 2,) + chunk, bf16),
            pltpu.SemaphoreType.DMA((9,)),
            pltpu.SemaphoreType.DMA((9,)),
            pltpu.SemaphoreType.DMA,
            pltpu.SemaphoreType.DMA((count,)),
            pltpu.SemaphoreType.DMA((count,)),
            pltpu.SemaphoreType.DMA((count - 2,)),
            pltpu.SemaphoreType.DMA((count - 2,)),
        ],
        compiler_params=pltpu.CompilerParams(
            collective_id=0, has_side_effects=True, vmem_limit_bytes=56 * 1024 * 1024
        ),
    )(v, vt, cx, cy, ce)


def local(eigen_modes, links_first, links_second):
    width = eigen_modes.shape[5]
    ng, ny, nm = lax.axis_size("gx"), lax.axis_size("gy"), lax.axis_size("ma")
    sites = eigen_modes.shape[2] * eigen_modes.shape[3]
    rows = width * nm // (ng * ny)
    aligned = rows % 16 == 0 and width % (2 * rows) == 0 and sites % 16 == 0
    if ny == 2 and nm == 2 and ng > 1 and aligned and eigen_modes.shape[1] > 2:
        return fused(eigen_modes, links_first, links_second)
    modes = jnp.transpose(eigen_modes, (0, 4, 1, 2, 3, 5))
    upper = shifted(modes[:, :, :1], "gx", -1)
    lower = shifted(modes[:, :, -1:], "gx", 1)
    lower_links = shifted(links_first[:, :, :, -1:], "gx", 1)
    lower_links_y = shifted(links_second[:, :, :, :, -1:], "gy", 1)
    field = modes.astype(jnp.float32)
    forward = jnp.concatenate([modes[:, :, 1:], upper], axis=2).astype(jnp.float32)
    linked = apply_link(links_first[:, :, :, :-1], field[:, :, :-1], True)
    behind = apply_link(lower_links, lower.astype(jnp.float32), True)
    backward = jnp.concatenate([behind, linked], axis=2)
    disp_x = (apply_link(links_first, forward, False) - backward).astype(jnp.bfloat16)
    upper_row = shifted(disp_x[:, :, :, :1], "gy", -1)
    lower_row = shifted(disp_x[:, :, :, -1:], "gy", 1)
    forward_y = jnp.concatenate([disp_x[:, :, :, 1:], upper_row], axis=3).astype(jnp.float32)
    linked_y = apply_link(links_second[:, :, :, :, :-1], disp_x[:, :, :, :-1].astype(jnp.float32), True)
    behind_y = apply_link(lower_links_y, lower_row.astype(jnp.float32), True)
    backward_y = jnp.concatenate([behind_y, linked_y], axis=3)
    disp_xy = (apply_link(links_second, forward_y, False) - backward_y).astype(jnp.bfloat16)
    right_x = disp_x.reshape(2, -1, width)
    right_y = disp_xy.reshape(2, -1, width)
    left = lax.all_gather(modes.reshape(2, -1, width), "ma", axis=2, tiled=True)
    outputs = []
    for right in (right_x, right_y):
        real_out = contract(left[0], right[0]) + contract(left[1], right[1])
        imag_out = contract(left[0], right[1]) - contract(left[1], right[0])
        outputs.append(jnp.stack([real_out, imag_out]))
    partial_terms = jnp.stack(outputs)
    across_x = lax.psum_scatter(partial_terms, "gx", scatter_dimension=2, tiled=True)
    return lax.psum_scatter(across_x, "gy", scatter_dimension=2, tiled=True)


def solution(mesh):
    return jax.shard_map(
        local,
        mesh=mesh,
        in_specs=(
            P("cuts", "gx", "gy", None, None, "ma"),
            P("cuts", None, None, "gx", "gy", None),
            P("cuts", None, None, "gx", "gy", None),
        ),
        out_specs=P("cuts", None, ("gx", "gy"), "ma"),
        check_vma=False,
    )
```

time: 93.5 us -> 41.2 us (0.44)
  local copies, waits for them, and re-layouts: 38.1 us -> 10.2 us
  other arithmetic: 24 us -> 0.1 us
  Pallas kernels: 21 us -> 30.7 us
  starting transfers between devices: 8.72 us -> 0 us
    mul x20 -> x0, local copies, waits for them, and re-layouts: 12.7 us -> none  [apply_link(): term_real = coef_real * field_real - factor * coef_imag * field_imag]
    another operation x8 -> x0, local copies, waits for them, and re-layouts: 11.7 us -> none  [apply_link(): return jnp.stack([jnp.stack(real_rows), jnp.stack(imag_rows)])]
    convert_element_type x14 -> x2, other arithmetic: 10 us -> 0.1 us  [coefs(): jnp.transpose(links, (3, 4, 5, 0, 1, 2)).reshape(planes, sites, 18)]
    pallas_call x1, Pallas kernels: 21 us -> 30.7 us  [fused(): pl.pallas_call(functools.partial(fused_kernel, nx), out_shape=jax.ShapeDt...]
    ppermute x7 -> x0, starting transfers between devices: 8.72 us -> none  [shifted(): return lax.ppermute(block, axis, route)]
    concatenate x4 -> x0, local copies, waits for them, and re-layouts: 6.24 us -> none  [the longest x2 3.61 us: local(): backward = jnp.concatenate([behind, linked], axis=2)]
    add x19 -> x0, other arithmetic: 5.55 us -> none  [the longest x18 5.46 us: apply_link(): real_acc = term_real if real_acc is None else real_acc + term_real]
    another operation x13 -> x0, other arithmetic: 3.49 us -> none  [apply_link(): return jnp.stack([jnp.stack(real_rows), jnp.stack(imag_rows)])]
  transfers between devices with their start and end apart: 7 -> 0, of which waited for: 0 -> 0; matrix products, arithmetic and copies ran while one was open for 57% -> 0% of each run, Pallas kernels for 0% -> 0%
where the time goes in v2:
time: 41.2 us; the launch traced here: 41 us
  Pallas kernels  30.7 us (75%)
  local copies, waits for them, and re-layouts  10.2 us (25%)
    pallas_call x1, Pallas kernels, fused(): pl.pallas_call(functools.partial(fused_kernel, nx), out_shape=jax.ShapeDt...  30.7 us
    transpose x1, local copies, waits for them, and re-layouts, fused(): jnp.transpose(eigen_modes, (0, 4, 1, 2, 3, 5))  1.98 us
    reshape x1, local copies, waits for them, and re-layouts, fused(): vt = jnp.transpose(eigen_modes, (0, 5, 4, 1, 2, 3)).reshape(2, width, depth)  1.84 us
    unnamed x9, local copies, waits for them, and re-layouts  1.7 us
    convert_element_type x4, local copies, waits for them, and re-layouts, coefs(): jnp.transpose(links, (3, 4, 5, 0, 1, 2)).reshape(planes, sites, 18)  1.58 us
    transpose x1, local copies, waits for them, and re-layouts, fused(): vt = jnp.transpose(eigen_modes, (0, 5, 4, 1, 2, 3)).reshape(2, width, depth)  1.22 us
    reshape x1, local copies, waits for them, and re-layouts, fused(): jnp.transpose(eigen_modes, (0, 4, 1, 2, 3, 5))  1.19 us

profile of v2, /device:TPU:0, one launch (start us, length us, event | category | flops | bytes accessed | tf_op | source)
XLA Modules:
  0.0 41.0 jit_solution(5208750494077417679)
XLA Ops:
  0.0 2.0 %copy.8 = bf16[2,3,8,16,2,256]{5,4,3,2,1,0:T(2,128)(2,1)S(1)} copy(bf16[2,3,8,16,2,256]{5,4,1,3,2,0:T(2,128)(2,1)} %bitcast.9) | data formatting | bytes 1572864 | tf_op jit(solution)/shard_map/transpose | solution.py:277
  2.0 0.0 copy-start
  2.0 1.2 %reshape.12.v_ref = bf16[2,3,8,32,256]{4,3,2,1,0:T(8,128)(2,1)} reshape(bf16[2,3,8,16,2,256]{5,4,3,2,1,0:T(2,128)(2,1)S(1)} %copy.8) | data formatting | bytes 1572864 | tf_op jit(solution)/shard_map/reshape | solution.py:277
  3.2 0.0 copy-done
  3.2 1.2 %copy.9 = bf16[2,256,3,8,16,2]{1,0,5,4,3,2:T(2,128)(2,1)S(1)} copy(bf16[2,256,3,8,16,2]{1,5,2,4,3,0:T(2,128)(2,1)S(1)} %bitcast.10) | data formatting | bytes 1572864 | tf_op jit(solution)/shard_map/transpose | solution.py:278
  4.4 0.0 copy-start.2
  4.4 1.8 %copy.13.vt_ref = bf16[2,256,768]{2,1,0:T(8,128)(2,1)} copy(bf16[2,256,768]{1,0,2:T(2,128)(2,1)S(1)} %bitcast.11) | data formatting | bytes 1572864 | tf_op jit(solution)/shard_map/reshape | solution.py:278
  6.3 0.0 copy-done.2
  6.3 0.1 convert_bitcast_fusion.1
  6.3 0.2 copy.10
  6.5 0.0 copy-start.3
  6.5 0.9 %copy.14.cx_ref = f32[8,32,18]{2,1,0:T(8,128)} copy(f32[8,32,18]{0,1,2:T(8,128)S(1)} %bitcast.12) | data formatting | bytes 36864 | tf_op jit(solution)/shard_map/convert_element_type | solution.py:281
  7.5 0.0 copy-done.3
  7.5 0.1 convert_bitcast_fusion
  7.5 0.2 copy.11
  7.7 0.3 copy.15.cy_ref
  8.0 0.0 copy-start.1
  8.0 0.7 %slice.4.ce_ref = f32[8,2,18]{2,1,0:T(2,128)} slice(f32[8,32,18]{2,1,0:T(8,128)S(1)} %copy.15.cy_ref), slice={[0:8], [30:32], [0:18]} | slice | bytes 2304 | tf_op jit(solution)/shard_map/slice | solution.py:285
  8.7 0.0 copy-done.1
  8.7 30.7 %shard_map.37 = f32[2,2,64,256]{3,2,1,0:T(8,128)} custom-call(bf16[2,3,8,32,256]{4,3,2,1,0:T(8,128)(2,1)} %reshape.12.v_ref, bf16[2,256,768]{2,1,0:T(8,128)(2,1)} %copy.13.vt_ref, f32[8,32,18]{2,1,0:T(8,128)} %copy.14.cx_ref, f32[8,32,18]{2,1,0:T(8,128)} %copy-done.1, f32[8,2,18]{2,1,0:T(2,128)} %slice.4.ce_ref), custom_call_target="tpu_custom_call" | custom-call | tf_op jit(solution)/shard_map/pallas_call | solution.py:292
  39.4 1.7 %copy.17 = f32[2,2,64,256]{3,2,1,0:T(8,128)} copy(f32[2,2,64,256]{3,2,1,0:T(8,128)} %shard_map.37) | data formatting | bytes 524288
Async XLA Ops:
  2.0 1.2 %copy-start = (bf16[2,8,16,2,3,256]{5,3,4,2,1,0:T(2,128)(2,1)S(1)}, bf16[2,8,16,2,3,256]{5,3,4,2,1,0:T(2,128)(2,1)}, u32[]{:S(2)}) copy-start(bf16[2,8,16,2,3,256]{5,3,4,2,1,0:T(2,128)(2,1)} %param.3) | copy-start | bytes 2359300
  4.4 1.9 %copy-start.2 = (bf16[2,3,3,8,16,2]{4,5,3,2,1,0:T(2,128)(2,1)S(1)}, bf16[2,3,3,8,16,2]{4,5,3,2,1,0:T(2,128)(2,1)}, u32[]{:S(2)}) copy-start(bf16[2,3,3,8,16,2]{4,5,3,2,1,0:T(2,128)(2,1)} %param.4) | copy-start | bytes 27652
  6.5 1.0 %copy-start.3 = (bf16[2,3,3,8,16,2]{4,5,3,2,1,0:T(2,128)(2,1)S(1)}, bf16[2,3,3,8,16,2]{4,5,3,2,1,0:T(2,128)(2,1)}, u32[]{:S(2)}) copy-start(bf16[2,3,3,8,16,2]{4,5,3,2,1,0:T(2,128)(2,1)} %param.5) | copy-start | bytes 27652
  8.0 0.7 %copy-start.1 = (f32[8,32,18]{2,1,0:T(8,128)}, f32[8,32,18]{2,1,0:T(8,128)S(1)}, u32[]{:S(2)}) copy-start(f32[8,32,18]{2,1,0:T(8,128)S(1)} %copy.15.cy_ref) | copy-start | bytes 55300

commit v3 on v2

--- a/solution.py
+++ b/solution.py
@@ -49,13 +49,13 @@
     )
 
 
-def linked(coefs, real, imag, dagger):
+def linked(coefs, real, imag, dagger, first=0):
     shape = real[0].shape
     outs_real, outs_imag = [], []
     for row in range(3):
         acc_real = acc_imag = None
         for col in range(3):
-            k = 3 * col + row if dagger else 3 * row + col
+            k = first + (3 * col + row if dagger else 3 * row + col)
             cr = jnp.broadcast_to(coefs[:, k : k + 1], shape)
             ci = jnp.broadcast_to(coefs[:, 9 + k : 10 + k], shape)
             if dagger:
@@ -71,17 +71,17 @@
     return outs_real + outs_imag
 
 
-def fused_kernel(nx, v_ref, vt_ref, cx_ref, cy_ref, ce_ref, out_ref,
-                 left, rx, ry, wx, fy, wy, hup, hlo, chx, chy, ysend, yrecv,
+def fused_kernel(nx, v_ref, cf_ref, out_ref,
+                 left, vs, ce, hupraw, hloraw, rx, ry, wx, fy, wy, hup, hlo, chx, chy, ysend, yrecv,
                  own, xsend, xrecv, zsend, zrecv,
-                 hs_sem, hr_sem, l_sem, xs_sem, xr_sem, zs_sem, zr_sem):
+                 hs_sem, hr_sem, xs_sem, xr_sem, zs_sem, zr_sem):
     gx = lax.axis_index("gx")
     gy = lax.axis_index("gy")
     ma = lax.axis_index("ma")
     other = 1 - gy
     rows = out_ref.shape[2]
-    planes, sites, width = v_ref.shape[2:]
-    zdim = ce_ref.shape[1]
+    _, _, planes, sites, width = vs.shape
+    zdim = ce.shape[1]
     f32 = jnp.float32
     tile = 16
     up, down = lax.rem(gx + 1, nx), lax.rem(gx + nx - 1, nx)
@@ -103,13 +103,25 @@
         copy.start()
         return copy
 
-    copy_down = send(0, v_ref.at[:, :, 0], hup, {"gx": down})
-    copy_up = send(1, v_ref.at[:, :, planes - 1], hlo, {"gx": up})
-    copy_cx = send(2, cx_ref.at[planes - 1], chx, {"gx": up})
-    copy_cy = send(3, ce_ref, chy, {"gy": other})
-    copy_vt = send(4, vt_ref, left.at[ma], {"ma": 1 - ma})
-    copy_own = pltpu.make_async_copy(vt_ref, left.at[ma], l_sem)
-    copy_own.start()
+    copy_up = send(1, v_ref.at[:, planes - 1], hloraw, {"gx": up})
+    copy_cx = send(2, cf_ref.at[planes - 1], chx, {"gx": up})
+    copy_down = send(0, v_ref.at[:, 0], hupraw, {"gx": down})
+    for x in range(planes):
+        ce[x] = cf_ref[x, sites - zdim :]
+
+    def relay(x, carry):
+        for p in range(2):
+            for c in range(3):
+                vs[p, c, x] = v_ref[p, x, :, c].reshape(sites, width)
+        return carry
+
+    lax.fori_loop(0, planes, relay, 0)
+    copy_cy = send(3, ce, chy, {"gy": other})
+    span = planes * sites
+    for p in range(2):
+        for c in range(3):
+            left[ma, p, :, c * span : (c + 1) * span] = vs[p, c].reshape(span, width).T
+    copy_vt = send(4, left.at[ma], left.at[ma], {"ma": 1 - ma})
 
     def part(t):
         return pl.ds(t * tile, tile)
@@ -136,15 +148,15 @@
                 ysend[1, edge_slot, i] = wide[tile - zdim :].astype(ysend.dtype)
 
     def plane(x):
-        return lambda p, c, t: v_ref[p, c, x, part(t)]
+        return lambda p, c, t: vs[p, c, x, part(t)]
 
     tiles = range(sites // tile)
     for t in tiles:
-        back_x(cx_ref[0, part(t)], plane(0), 1, t)
+        back_x(cf_ref[0, part(t)], plane(0), 1, t)
 
     def inner(x, carry):
         for t in tiles:
-            coefs = cx_ref[x, part(t)]
+            coefs = cf_ref[x, part(t)]
             back_x(coefs, plane(x), x + 1, t)
             fore_x(x, coefs, plane(x + 1), x - 1, t)
         return carry
@@ -158,12 +170,18 @@
     ]
     copy_cx.wait()
     copy_up.wait()
+    for p in range(2):
+        for c in range(3):
+            hlo[p, c] = hloraw[p, :, c].reshape(sites, width)
     for t in tiles:
         back_x(chx[part(t)], lambda p, c, t: hlo[p, c, part(t)], 0, t)
-        fore_x(0, cx_ref[0, part(t)], plane(1), inner_edges, t)
+        fore_x(0, cf_ref[0, part(t)], plane(1), inner_edges, t)
     copy_down.wait()
+    for p in range(2):
+        for c in range(3):
+            hup[p, c] = hupraw[p, :, c].reshape(sites, width)
     for t in tiles:
-        fore_x(planes - 1, cx_ref[planes - 1, part(t)],
+        fore_x(planes - 1, cf_ref[planes - 1, part(t)],
                lambda p, c, t: hup[p, c, part(t)], inner_edges + 1, t)
     copies_y += [
         send(7 + s, ysend.at[s, pl.ds(inner_edges, 2)], yrecv.at[s, pl.ds(inner_edges, 2)],
@@ -171,7 +189,6 @@
         for s in range(2)
     ]
     copy_vt.wait()
-    copy_own.wait()
 
     offsets = sorted(range(1, nx), key=lambda o: -min(o, nx - o)) + [0]
     rights = (rx, ry)
@@ -232,17 +249,17 @@
             fy[i, pad : pad + sites] = rx[i // 3, i % 3, x].astype(f32)
             fy[i, pad + sites : pad + sites + zdim] = yrecv[0, slot, i].astype(f32)
         low = [yrecv[1, slot, i].astype(f32) for i in range(6)]
-        values = linked(chy[x], low[:3], low[3:], True)
+        values = linked(chy[x], low[:3], low[3:], True, 18)
         for i in range(6):
             wy[i, pad - zdim : pad] = values[i]
         for t in tiles:
-            coefs = cy_ref[x, part(t)]
+            coefs = cf_ref[x, part(t)]
             here = [fy[i, pad + t * tile : pad + (t + 1) * tile] for i in range(6)]
-            values = linked(coefs, here[:3], here[3:], True)
+            values = linked(coefs, here[:3], here[3:], True, 18)
             for i in range(6):
                 wy[i, pad + t * tile : pad + (t + 1) * tile] = values[i]
             ahead = [fy[i, pad + zdim + t * tile : pad + zdim + (t + 1) * tile] for i in range(6)]
-            values = linked(coefs, ahead[:3], ahead[3:], False)
+            values = linked(coefs, ahead[:3], ahead[3:], False, 18)
             for i in range(6):
                 behind = wy[i, pad - zdim + t * tile : pad - zdim + (t + 1) * tile]
                 ry[i // 3, i % 3, x, part(t)] = (values[i] - behind).astype(ry.dtype)
@@ -274,28 +291,26 @@
     _, planes, ysize, zdim, _, width = eigen_modes.shape
     sites = ysize * zdim
     depth = 3 * planes * sites
-    v = jnp.transpose(eigen_modes, (0, 4, 1, 2, 3, 5)).reshape(2, 3, planes, sites, width)
-    vt = jnp.transpose(eigen_modes, (0, 5, 4, 1, 2, 3)).reshape(2, width, depth)
-
-    def coefs(links):
-        return jnp.transpose(links, (3, 4, 5, 0, 1, 2)).reshape(planes, sites, 18).astype(jnp.float32)
-
-    cx = coefs(links_first)
-    cy = coefs(links_second)
-    ce = cy[:, sites - zdim :]
+    v = jnp.transpose(eigen_modes, (0, 1, 2, 4, 3, 5))
+    links = jnp.stack([links_first, links_second])
+    cf = jnp.transpose(links, (4, 5, 6, 0, 1, 2, 3)).reshape(planes, sites, 36)
+    cf = cf.astype(jnp.float32)
     rows = width * nm // (nx * ny)
     count = 2 * nx
     bf16, f32 = jnp.bfloat16, jnp.float32
     vmem = pl.BlockSpec(memory_space=pltpu.VMEM)
     chunk = (2, rows, width)
-    edges = 2 * 2
     return pl.pallas_call(
         functools.partial(fused_kernel, nx),
         out_shape=jax.ShapeDtypeStruct((2, 2, rows, width), f32),
-        in_specs=[vmem] * 5,
+        in_specs=[vmem] * 2,
         out_specs=vmem,
         scratch_shapes=[
             pltpu.VMEM((nm, 2, width, depth), bf16),
+            pltpu.VMEM((2, 3, planes, sites, width), bf16),
+            pltpu.VMEM((planes, zdim, 36), f32),
+            pltpu.VMEM((2, ysize, 3, zdim, width), bf16),
+            pltpu.VMEM((2, ysize, 3, zdim, width), bf16),
             pltpu.VMEM((2, 3, planes, sites, width), bf16),
             pltpu.VMEM((2, 3, planes, sites, width), bf16),
             pltpu.VMEM((planes, 6, sites, width), f32),
@@ -303,8 +318,8 @@
             pltpu.VMEM((6, sites + 16, width), f32),
             pltpu.VMEM((2, 3, sites, width), bf16),
             pltpu.VMEM((2, 3, sites, width), bf16),
-            pltpu.VMEM((sites, 18), f32),
-            pltpu.VMEM((planes, zdim, 18), f32),
+            pltpu.VMEM((sites, 36), f32),
+            pltpu.VMEM((planes, zdim, 36), f32),
             pltpu.VMEM((2, planes, 6, zdim, width), bf16),
             pltpu.VMEM((2, planes, 6, zdim, width), bf16),
             pltpu.VMEM((count,) + chunk, f32),
@@ -314,16 +329,15 @@
             pltpu.VMEM((count - 2,) + chunk, bf16),
             pltpu.SemaphoreType.DMA((9,)),
             pltpu.SemaphoreType.DMA((9,)),
-            pltpu.SemaphoreType.DMA,
             pltpu.SemaphoreType.DMA((count,)),
             pltpu.SemaphoreType.DMA((count,)),
             pltpu.SemaphoreType.DMA((count - 2,)),
             pltpu.SemaphoreType.DMA((count - 2,)),
         ],
         compiler_params=pltpu.CompilerParams(
-            collective_id=0, has_side_effects=True, vmem_limit_bytes=56 * 1024 * 1024
+            collective_id=0, has_side_effects=True, vmem_limit_bytes=24 * 1024 * 1024
         ),
-    )(v, vt, cx, cy, ce)
+    )(v, cf)
 
 
 def local(eigen_modes, links_first, links_second):

time: 41.2 us -> 31.7 us (0.77)
  local copies, waits for them, and re-layouts: 10.2 us -> 1.82 us
  Pallas kernels: 30.7 us -> 28.5 us
  other arithmetic: 0.1 us -> 1.14 us
    transpose x2 -> x0, local copies, waits for them, and re-layouts: 3.2 us -> none  [the longest x1 1.98 us: fused(): jnp.transpose(eigen_modes, (0, 4, 1, 2, 3, 5))]
    reshape x2 -> x0, local copies, waits for them, and re-layouts: 3.03 us -> none  [the longest x1 1.84 us: fused(): vt = jnp.transpose(eigen_modes, (0, 5, 4, 1, 2, 3)).reshape(2, width, depth)]
    pallas_call x1, Pallas kernels: 30.7 us -> 28.5 us  [fused(): pl.pallas_call(functools.partial(fused_kernel, nx), out_shape=jax.ShapeDt...]
    convert_element_type x2 -> x1, other arithmetic: 0.1 us -> 1.14 us  [fused(): cf = cf.astype(jnp.float32)]
    unnamed x9 -> x3, local copies, waits for them, and re-layouts: 1.7 us -> 0.94 us
    convert_element_type x4 -> x2, local copies, waits for them, and re-layouts: 1.58 us -> 0.88 us  [fused(): cf = cf.astype(jnp.float32)]
    slice x1 -> x0, local copies, waits for them, and re-layouts: 0.66 us -> none  [fused(): ce = cy[:, sites - zdim:]]
where the time goes in v3:
time: 31.7 us; the launch traced here: 31.5 us
  Pallas kernels  28.5 us (90%)
  local copies, waits for them, and re-layouts  1.82 us (6%)
  other arithmetic  1.14 us (4%)
    pallas_call x1, Pallas kernels, fused(): pl.pallas_call(functools.partial(fused_kernel, nx), out_shape=jax.ShapeDt...  28.5 us
    convert_element_type x1, other arithmetic, fused(): cf = cf.astype(jnp.float32)  1.14 us
    unnamed x3, local copies, waits for them, and re-layouts  0.94 us
    convert_element_type x2, local copies, waits for them, and re-layouts, fused(): cf = cf.astype(jnp.float32)  0.88 us

profile of v3, /device:TPU:0, one launch (start us, length us, event | category | flops | bytes accessed | tf_op | source)
XLA Modules:
  0.0 31.5 jit_solution(11226716383153920209)
XLA Ops:
  0.0 1.1 %convert_bitcast_fusion = f32[8,16,2,2,2,3,3]{1,2,0,6,5,4,3:T(2,128)S(1)} fusion(bf16[1,2,3,3,8,16,2]{5,6,4,3,2,1,0:T(2,128)(2,1)} %bitcast.8, bf16[1,2,3,3,8,16,2]{5,6,4,3,2,1,0:T(2,128)(2,1)} %bitcast.9), kind=kLoop, calls=%fused_computation | loop fusion | flops 18432 | bytes 55296 | tf_op jit(solution)/shard_map/convert_element_type | solution.py:297
  1.1 0.0 copy-start
  1.2 0.4 %copy.5 = f32[8,16,2,2,2,3,3]{0,2,1,6,5,4,3:T(2,128)S(1)} copy(f32[8,16,2,2,2,3,3]{1,2,0,6,5,4,3:T(2,128)S(1)} %convert_bitcast_fusion) | data formatting | bytes 73728 | tf_op jit(solution)/shard_map/convert_element_type | solution.py:297
  1.6 0.5 %copy.6.cf_ref = f32[8,32,36]{2,1,0:T(8,128)S(1)} copy(f32[8,32,36]{0,1,2:T(8,128)S(1)} %bitcast.7) | data formatting | bytes 73728 | tf_op jit(solution)/shard_map/convert_element_type | solution.py:297
  2.0 0.2 copy-done
  2.3 28.5 %shard_map.37 = f32[2,2,64,256]{3,2,1,0:T(8,128)S(1)} custom-call(bf16[2,8,16,3,2,256]{5,4,3,2,1,0:T(2,128)(2,1)S(1)} %bitcast.6, f32[8,32,36]{2,1,0:T(8,128)S(1)} %copy.6.cf_ref), custom_call_target="tpu_custom_call" | custom-call | tf_op jit(solution)/shard_map/pallas_call | solution.py:303
  30.8 0.7 %copy.8 = f32[2,2,64,256]{3,2,1,0:T(8,128)} copy(f32[2,2,64,256]{3,2,1,0:T(8,128)S(1)} %shard_map.37) | data formatting | bytes 524288
Async XLA Ops:
  1.1 1.1 %copy-start = (bf16[2,8,16,2,3,256]{5,3,4,2,1,0:T(2,128)(2,1)S(1)}, bf16[2,8,16,2,3,256]{5,3,4,2,1,0:T(2,128)(2,1)}, u32[]{:S(2)}) copy-start(bf16[2,8,16,2,3,256]{5,3,4,2,1,0:T(2,128)(2,1)} %param.3) | copy-start | bytes 2359300

commit v4 on v3

--- a/solution.py
+++ b/solution.py
@@ -49,13 +49,13 @@
     )
 
 
-def linked(coefs, real, imag, dagger, first=0):
+def linked(coefs, real, imag, dagger):
     shape = real[0].shape
     outs_real, outs_imag = [], []
     for row in range(3):
         acc_real = acc_imag = None
         for col in range(3):
-            k = first + (3 * col + row if dagger else 3 * row + col)
+            k = 3 * col + row if dagger else 3 * row + col
             cr = jnp.broadcast_to(coefs[:, k : k + 1], shape)
             ci = jnp.broadcast_to(coefs[:, 9 + k : 10 + k], shape)
             if dagger:
@@ -71,8 +71,8 @@
     return outs_real + outs_imag
 
 
-def fused_kernel(nx, v_ref, cf_ref, out_ref,
-                 left, vs, ce, hupraw, hloraw, rx, ry, wx, fy, wy, hup, hlo, chx, chy, ysend, yrecv,
+def fused_kernel(nx, v_ref, l1_ref, l2_ref, out_ref,
+                 left, vs, cf, cf2, ce, hupraw, hloraw, rx, ry, wx, fy, wy, hup, hlo, chx, chy, ysend, yrecv,
                  own, xsend, xrecv, zsend, zrecv,
                  hs_sem, hr_sem, xs_sem, xr_sem, zs_sem, zr_sem):
     gx = lax.axis_index("gx")
@@ -93,6 +93,30 @@
         )
     pl.semaphore_signal(barrier, inc=1, device_id={"gy": other}, device_id_type=MESH)
     pl.semaphore_signal(barrier, inc=1, device_id={"ma": 1 - ma}, device_id_type=MESH)
+
+    sel_row = lax.broadcasted_iota(jnp.int32, (sites, sites // zdim), 0)
+    sel_col = lax.broadcasted_iota(jnp.int32, (sites, sites // zdim), 1)
+    picks = [(sel_row == sel_col * zdim + z).astype(jnp.bfloat16) for z in range(zdim)]
+
+    def relay(x, carry):
+        for source, target in ((l1_ref, cf), (l2_ref, cf2)):
+            raw = source[:, x].astype(f32)
+            total = None
+            for z in range(zdim):
+                term = lax.dot_general(
+                    picks[z], raw[:, z, :].astype(jnp.bfloat16),
+                    (((1,), (1,)), ((), ())), preferred_element_type=f32,
+                )
+                total = term if total is None else total + term
+            target[x] = total
+            if source is l2_ref:
+                ce[x] = total[sites - zdim :]
+        for p in range(2):
+            for c in range(3):
+                vs[p, c, x] = v_ref[p, x, :, c].reshape(sites, width)
+        return carry
+
+    lax.fori_loop(0, planes, relay, 0)
     pl.semaphore_wait(barrier, nx + 1)
 
     def send(i, src, dst, target):
@@ -104,18 +128,8 @@
         return copy
 
     copy_up = send(1, v_ref.at[:, planes - 1], hloraw, {"gx": up})
-    copy_cx = send(2, cf_ref.at[planes - 1], chx, {"gx": up})
+    copy_cx = send(2, cf.at[planes - 1], chx, {"gx": up})
     copy_down = send(0, v_ref.at[:, 0], hupraw, {"gx": down})
-    for x in range(planes):
-        ce[x] = cf_ref[x, sites - zdim :]
-
-    def relay(x, carry):
-        for p in range(2):
-            for c in range(3):
-                vs[p, c, x] = v_ref[p, x, :, c].reshape(sites, width)
-        return carry
-
-    lax.fori_loop(0, planes, relay, 0)
     copy_cy = send(3, ce, chy, {"gy": other})
     span = planes * sites
     for p in range(2):
@@ -152,11 +166,11 @@
 
     tiles = range(sites // tile)
     for t in tiles:
-        back_x(cf_ref[0, part(t)], plane(0), 1, t)
+        back_x(cf[0, part(t)], plane(0), 1, t)
 
     def inner(x, carry):
         for t in tiles:
-            coefs = cf_ref[x, part(t)]
+            coefs = cf[x, part(t)]
             back_x(coefs, plane(x), x + 1, t)
             fore_x(x, coefs, plane(x + 1), x - 1, t)
         return carry
@@ -175,13 +189,13 @@
             hlo[p, c] = hloraw[p, :, c].reshape(sites, width)
     for t in tiles:
         back_x(chx[part(t)], lambda p, c, t: hlo[p, c, part(t)], 0, t)
-        fore_x(0, cf_ref[0, part(t)], plane(1), inner_edges, t)
+        fore_x(0, cf[0, part(t)], plane(1), inner_edges, t)
     copy_down.wait()
     for p in range(2):
         for c in range(3):
             hup[p, c] = hupraw[p, :, c].reshape(sites, width)
     for t in tiles:
-        fore_x(planes - 1, cf_ref[planes - 1, part(t)],
+        fore_x(planes - 1, cf[planes - 1, part(t)],
                lambda p, c, t: hup[p, c, part(t)], inner_edges + 1, t)
     copies_y += [
         send(7 + s, ysend.at[s, pl.ds(inner_edges, 2)], yrecv.at[s, pl.ds(inner_edges, 2)],
@@ -249,17 +263,17 @@
             fy[i, pad : pad + sites] = rx[i // 3, i % 3, x].astype(f32)
             fy[i, pad + sites : pad + sites + zdim] = yrecv[0, slot, i].astype(f32)
         low = [yrecv[1, slot, i].astype(f32) for i in range(6)]
-        values = linked(chy[x], low[:3], low[3:], True, 18)
+        values = linked(chy[x], low[:3], low[3:], True)
         for i in range(6):
             wy[i, pad - zdim : pad] = values[i]
         for t in tiles:
-            coefs = cf_ref[x, part(t)]
+            coefs = cf2[x, part(t)]
             here = [fy[i, pad + t * tile : pad + (t + 1) * tile] for i in range(6)]
-            values = linked(coefs, here[:3], here[3:], True, 18)
+            values = linked(coefs, here[:3], here[3:], True)
             for i in range(6):
                 wy[i, pad + t * tile : pad + (t + 1) * tile] = values[i]
             ahead = [fy[i, pad + zdim + t * tile : pad + zdim + (t + 1) * tile] for i in range(6)]
-            values = linked(coefs, ahead[:3], ahead[3:], False, 18)
+            values = linked(coefs, ahead[:3], ahead[3:], False)
             for i in range(6):
                 behind = wy[i, pad - zdim + t * tile : pad - zdim + (t + 1) * tile]
                 ry[i // 3, i % 3, x, part(t)] = (values[i] - behind).astype(ry.dtype)
@@ -292,9 +306,10 @@
     sites = ysize * zdim
     depth = 3 * planes * sites
     v = jnp.transpose(eigen_modes, (0, 1, 2, 4, 3, 5))
-    links = jnp.stack([links_first, links_second])
-    cf = jnp.transpose(links, (4, 5, 6, 0, 1, 2, 3)).reshape(planes, sites, 36)
-    cf = cf.astype(jnp.float32)
+
+    def raw(links):
+        return jnp.transpose(links, (0, 1, 2, 3, 5, 4)).reshape(18, planes, zdim, ysize)
+
     rows = width * nm // (nx * ny)
     count = 2 * nx
     bf16, f32 = jnp.bfloat16, jnp.float32
@@ -303,12 +318,14 @@
     return pl.pallas_call(
         functools.partial(fused_kernel, nx),
         out_shape=jax.ShapeDtypeStruct((2, 2, rows, width), f32),
-        in_specs=[vmem] * 2,
+        in_specs=[vmem] * 3,
         out_specs=vmem,
         scratch_shapes=[
             pltpu.VMEM((nm, 2, width, depth), bf16),
             pltpu.VMEM((2, 3, planes, sites, width), bf16),
-            pltpu.VMEM((planes, zdim, 36), f32),
+            pltpu.VMEM((planes, sites, 18), f32),
+            pltpu.VMEM((planes, sites, 18), f32),
+            pltpu.VMEM((planes, zdim, 18), f32),
             pltpu.VMEM((2, ysize, 3, zdim, width), bf16),
             pltpu.VMEM((2, ysize, 3, zdim, width), bf16),
             pltpu.VMEM((2, 3, planes, sites, width), bf16),
@@ -318,8 +335,8 @@
             pltpu.VMEM((6, sites + 16, width), f32),
             pltpu.VMEM((2, 3, sites, width), bf16),
             pltpu.VMEM((2, 3, sites, width), bf16),
-            pltpu.VMEM((sites, 36), f32),
-            pltpu.VMEM((planes, zdim, 36), f32),
+            pltpu.VMEM((sites, 18), f32),
+            pltpu.VMEM((planes, zdim, 18), f32),
             pltpu.VMEM((2, planes, 6, zdim, width), bf16),
             pltpu.VMEM((2, planes, 6, zdim, width), bf16),
             pltpu.VMEM((count,) + chunk, f32),
@@ -337,7 +354,7 @@
         compiler_params=pltpu.CompilerParams(
             collective_id=0, has_side_effects=True, vmem_limit_bytes=24 * 1024 * 1024
         ),
-    )(v, cf)
+    )(v, raw(links_first), raw(links_second))
 
 
 def local(eigen_modes, links_first, links_second):

time: 31.7 us -> 32.6 us (1.028)
  local copies, waits for them, and re-layouts: 1.82 us -> 3.61 us
  other arithmetic: 1.14 us -> 0 us
    unnamed x3 -> x7, local copies, waits for them, and re-layouts: 0.94 us -> 3.61 us
    convert_element_type x1 -> x0, other arithmetic: 1.14 us -> none  [fused(): cf = cf.astype(jnp.float32)]
    convert_element_type x2 -> x0, local copies, waits for them, and re-layouts: 0.88 us -> none  [fused(): cf = cf.astype(jnp.float32)]
where the time goes in v4:
time: 32.6 us; the launch traced here: 32.4 us
  Pallas kernels  28.8 us (88%)
  local copies, waits for them, and re-layouts  3.61 us (11%)
    pallas_call x1, Pallas kernels, fused(): pl.pallas_call(functools.partial(fused_kernel, nx), out_shape=jax.ShapeDt...  28.8 us
    unnamed x7, local copies, waits for them, and re-layouts  3.61 us

profile of v4, /device:TPU:0, one launch (start us, length us, event | category | flops | bytes accessed | tf_op | source)
XLA Modules:
  0.0 32.4 jit_solution(6109427975901685404)
XLA Ops:
  0.0 0.0 copy-start
  0.0 1.1 %copy-done = bf16[2,8,16,2,3,256]{5,3,4,2,1,0:T(2,128)(2,1)S(1)} copy-done((bf16[2,8,16,2,3,256]{5,3,4,2,1,0:T(2,128)(2,1)S(1)}, bf16[2,8,16,2,3,256]{5,3,4,2,1,0:T(2,128)(2,1)}, u32[]{:S(2)}) %copy-start) | copy-done | bytes 786456
  1.1 0.0 copy-start.1
  1.1 0.9 %copy-done.1 = bf16[2,3,3,8,16,2]{4,5,3,2,1,0:T(2,128)(2,1)S(1)} copy-done((bf16[2,3,3,8,16,2]{4,5,3,2,1,0:T(2,128)(2,1)S(1)}, bf16[2,3,3,8,16,2]{4,5,3,2,1,0:T(2,128)(2,1)}, u32[]{:S(2)}) %copy-start.1) | copy-done | bytes 9240
  2.0 0.0 copy-start.2
  2.0 0.9 %copy-done.2 = bf16[2,3,3,8,16,2]{4,5,3,2,1,0:T(2,128)(2,1)S(1)} copy-done((bf16[2,3,3,8,16,2]{4,5,3,2,1,0:T(2,128)(2,1)S(1)}, bf16[2,3,3,8,16,2]{4,5,3,2,1,0:T(2,128)(2,1)}, u32[]{:S(2)}) %copy-start.2) | copy-done | bytes 9240
  2.9 28.8 %shard_map.37 = f32[2,2,64,256]{3,2,1,0:T(8,128)S(1)} custom-call(bf16[2,8,16,3,2,256]{5,4,3,2,1,0:T(2,128)(2,1)S(1)} %bitcast.7, bf16[18,8,2,16]{3,2,1,0:T(2,128)(2,1)S(1)} %bitcast.8, bf16[18,8,2,16]{3,2,1,0:T(2,128)(2,1)S(1)} %bitcast.9), custom_call_target="tpu_custom_call" | custom-call | tf_op jit(solution)/shard_map/pallas_call | solution.py:318
  31.7 0.7 %copy.5 = f32[2,2,64,256]{3,2,1,0:T(8,128)} copy(f32[2,2,64,256]{3,2,1,0:T(8,128)S(1)} %shard_map.37) | data formatting | bytes 524288
Async XLA Ops:
  0.0 1.1 %copy-start = (bf16[2,8,16,2,3,256]{5,3,4,2,1,0:T(2,128)(2,1)S(1)}, bf16[2,8,16,2,3,256]{5,3,4,2,1,0:T(2,128)(2,1)}, u32[]{:S(2)}) copy-start(bf16[2,8,16,2,3,256]{5,3,4,2,1,0:T(2,128)(2,1)} %param.3) | copy-start | bytes 2359300
  1.1 0.9 %copy-start.1 = (bf16[2,3,3,8,16,2]{4,5,3,2,1,0:T(2,128)(2,1)S(1)}, bf16[2,3,3,8,16,2]{4,5,3,2,1,0:T(2,128)(2,1)}, u32[]{:S(2)}) copy-start(bf16[2,3,3,8,16,2]{4,5,3,2,1,0:T(2,128)(2,1)} %param.4) | copy-start | bytes 27652
  2.0 0.9 %copy-start.2 = (bf16[2,3,3,8,16,2]{4,5,3,2,1,0:T(2,128)(2,1)S(1)}, bf16[2,3,3,8,16,2]{4,5,3,2,1,0:T(2,128)(2,1)}, u32[]{:S(2)}) copy-start(bf16[2,3,3,8,16,2]{4,5,3,2,1,0:T(2,128)(2,1)} %param.5) | copy-start | bytes 27652

commit v5 on v4

--- a/solution.py
+++ b/solution.py
@@ -71,10 +71,10 @@
     return outs_real + outs_imag
 
 
-def fused_kernel(nx, v_ref, l1_ref, l2_ref, out_ref,
-                 left, vs, cf, cf2, ce, hupraw, hloraw, rx, ry, wx, fy, wy, hup, hlo, chx, chy, ysend, yrecv,
+def fused_kernel(nx, v_hbm, l1_hbm, l2_hbm, out_ref,
+                 v_ref, l1_ref, l2_ref, left, vs, cf, cf2, ce, hupraw, hloraw, rx, ry, wx, fy, wy, hup, hlo, chx, chy, ysend, yrecv,
                  own, xsend, xrecv, zsend, zrecv,
-                 hs_sem, hr_sem, xs_sem, xr_sem, zs_sem, zr_sem):
+                 in_sem, hs_sem, hr_sem, xs_sem, xr_sem, zs_sem, zr_sem):
     gx = lax.axis_index("gx")
     gy = lax.axis_index("gy")
     ma = lax.axis_index("ma")
@@ -86,11 +86,17 @@
     tile = 16
     up, down = lax.rem(gx + 1, nx), lax.rem(gx + nx - 1, nx)
 
+    staged = [
+        pltpu.make_async_copy(src, dst, in_sem.at[i])
+        for i, (src, dst) in enumerate(((v_hbm, v_ref), (l1_hbm, l1_ref), (l2_hbm, l2_ref)))
+    ]
     barrier = pltpu.get_barrier_semaphore()
     for off in range(1, nx):
         pl.semaphore_signal(
             barrier, inc=1, device_id={"gx": lax.rem(gx + off, nx)}, device_id_type=MESH
         )
+    for copy in staged:
+        copy.start()
     pl.semaphore_signal(barrier, inc=1, device_id={"gy": other}, device_id_type=MESH)
     pl.semaphore_signal(barrier, inc=1, device_id={"ma": 1 - ma}, device_id_type=MESH)
 
@@ -116,6 +122,8 @@
                 vs[p, c, x] = v_ref[p, x, :, c].reshape(sites, width)
         return carry
 
+    for copy in staged:
+        copy.wait()
     lax.fori_loop(0, planes, relay, 0)
     pl.semaphore_wait(barrier, nx + 1)
 
@@ -318,9 +326,12 @@
     return pl.pallas_call(
         functools.partial(fused_kernel, nx),
         out_shape=jax.ShapeDtypeStruct((2, 2, rows, width), f32),
-        in_specs=[vmem] * 3,
+        in_specs=[pl.BlockSpec(memory_space=pltpu.HBM)] * 3,
         out_specs=vmem,
         scratch_shapes=[
+            pltpu.VMEM((2, planes, ysize, 3, zdim, width), bf16),
+            pltpu.VMEM((18, planes, zdim, ysize), bf16),
+            pltpu.VMEM((18, planes, zdim, ysize), bf16),
             pltpu.VMEM((nm, 2, width, depth), bf16),
             pltpu.VMEM((2, 3, planes, sites, width), bf16),
             pltpu.VMEM((planes, sites, 18), f32),
@@ -344,6 +355,7 @@
             pltpu.VMEM((count,) + chunk, bf16),
             pltpu.VMEM((count - 2,) + chunk, bf16),
             pltpu.VMEM((count - 2,) + chunk, bf16),
+            pltpu.SemaphoreType.DMA((3,)),
             pltpu.SemaphoreType.DMA((9,)),
             pltpu.SemaphoreType.DMA((9,)),
             pltpu.SemaphoreType.DMA((count,)),
@@ -354,7 +366,7 @@
         compiler_params=pltpu.CompilerParams(
             collective_id=0, has_side_effects=True, vmem_limit_bytes=24 * 1024 * 1024
         ),
-    )(v, raw(links_first), raw(links_second))
+    )(*[pltpu.with_memory_space_constraint(a, pltpu.HBM) for a in (v, raw(links_first), raw(links_second))])
 
 
 def local(eigen_modes, links_first, links_second):

time: 32.6 us -> 30.7 us (0.942)
  local copies, waits for them, and re-layouts: 3.61 us -> 0.71 us
  Pallas kernels: 28.8 us -> 29.9 us
    unnamed x7 -> x1, local copies, waits for them, and re-layouts: 3.61 us -> 0.71 us
    pallas_call x1, Pallas kernels: 28.8 us -> 29.9 us  [fused(): pl.pallas_call(functools.partial(fused_kernel, nx), out_shape=jax.ShapeDt...]
where the time goes in v5:
time: 30.7 us; the launch traced here: 30.6 us
  Pallas kernels  29.9 us (97%)
  local copies, waits for them, and re-layouts  0.71 us (2%)
    pallas_call x1, Pallas kernels, fused(): pl.pallas_call(functools.partial(fused_kernel, nx), out_shape=jax.ShapeDt...  29.9 us
    unnamed x1, local copies, waits for them, and re-layouts  0.71 us

profile of v5, /device:TPU:0, one launch (start us, length us, event | category | flops | bytes accessed | tf_op | source)
XLA Modules:
  0.0 30.6 jit_solution(9090038114650281014)
XLA Ops:
  0.0 29.9 %shard_map.37 = f32[2,2,64,256]{3,2,1,0:T(8,128)S(1)} custom-call(bf16[2,8,16,3,2,256]{5,4,3,2,1,0:T(2,128)(2,1)} %bitcast.7, bf16[18,8,2,16]{3,2,1,0:T(2,128)(2,1)} %bitcast.8, bf16[18,8,2,16]{3,2,1,0:T(2,128)(2,1)} %bitcast.9), custom_call_target="tpu_custom_call" | custom-call | tf_op jit(solution)/shard_map/pallas_call | solution.py:326
  29.9 0.7 %copy.5 = f32[2,2,64,256]{3,2,1,0:T(8,128)} copy(f32[2,2,64,256]{3,2,1,0:T(8,128)S(1)} %shard_map.37) | data formatting | bytes 524288

commit v6 on v5

--- a/solution.py
+++ b/solution.py
@@ -91,10 +91,8 @@
         for i, (src, dst) in enumerate(((v_hbm, v_ref), (l1_hbm, l1_ref), (l2_hbm, l2_ref)))
     ]
     barrier = pltpu.get_barrier_semaphore()
-    for off in range(1, nx):
-        pl.semaphore_signal(
-            barrier, inc=1, device_id={"gx": lax.rem(gx + off, nx)}, device_id_type=MESH
-        )
+    for neighbour in (up, down):
+        pl.semaphore_signal(barrier, inc=1, device_id={"gx": neighbour}, device_id_type=MESH)
     for copy in staged:
         copy.start()
     pl.semaphore_signal(barrier, inc=1, device_id={"gy": other}, device_id_type=MESH)
@@ -122,10 +120,6 @@
                 vs[p, c, x] = v_ref[p, x, :, c].reshape(sites, width)
         return carry
 
-    for copy in staged:
-        copy.wait()
-    lax.fori_loop(0, planes, relay, 0)
-    pl.semaphore_wait(barrier, nx + 1)
 
     def send(i, src, dst, target):
         copy = pltpu.make_async_remote_copy(
@@ -135,9 +129,14 @@
         copy.start()
         return copy
 
+    staged[0].wait()
+    pl.semaphore_wait(barrier, 4)
     copy_up = send(1, v_ref.at[:, planes - 1], hloraw, {"gx": up})
+    copy_down = send(0, v_ref.at[:, 0], hupraw, {"gx": down})
+    for copy in staged[1:]:
+        copy.wait()
+    lax.fori_loop(0, planes, relay, 0)
     copy_cx = send(2, cf.at[planes - 1], chx, {"gx": up})
-    copy_down = send(0, v_ref.at[:, 0], hupraw, {"gx": down})
     copy_cy = send(3, ce, chy, {"gy": other})
     span = planes * sites
     for p in range(2):
@@ -212,7 +211,15 @@
     ]
     copy_vt.wait()
 
-    offsets = sorted(range(1, nx), key=lambda o: -min(o, nx - o)) + [0]
+    orders = [
+        sorted(range(nx), key=lambda t: (t == g, -abs(t - g))) for g in range(nx)
+    ]
+    targets = []
+    for step in range(nx):
+        target = orders[0][step]
+        for g in range(1, nx):
+            target = jnp.where(gx == g, orders[g][step], target)
+        targets.append(target)
     rights = (rx, ry)
     modes = left.shape[2]
     depth = left.shape[3]
@@ -221,7 +228,7 @@
 
     def project(k, d):
         c = 2 * k + d
-        base = lax.rem(gx + offsets[k], nx) * (2 * rows)
+        base = targets[k] * (2 * rows)
         half = base // modes
         start = pl.multiple_of(base - half * modes, 2 * rows)
         left_real = left[half, 0, pl.ds(start, 2 * rows), :]
@@ -242,18 +249,39 @@
         copy.start()
         x_copies[c] = copy
 
+    def arrived(c, side, slot):
+        pltpu.make_async_remote_copy(
+            src_ref=xsend.at[c], dst_ref=zrecv.at[side, slot],
+            send_sem=xs_sem.at[c], recv_sem=zr_sem.at[side, slot],
+            device_id={"gx": up}, device_id_type=MESH,
+        ).wait_recv()
+        own[c] = own[c] + zrecv[side, slot].astype(f32)
+
     def pass_on(k, d):
         c = 2 * k + d
+        target = targets[k]
+        slot = 2 * target + d
         x_copies[c].wait()
-        total = own[c] + xrecv[c].astype(f32)
-        if offsets[k] == 0:
-            own[c] = total
+        own[c] = own[c] + xrecv[c].astype(f32)
+
+        @pl.when(jnp.logical_and(gx > 0, target >= gx))
+        def _():
+            arrived(c, 0, slot)
+
+        @pl.when(jnp.logical_and(gx < nx - 1, target <= gx))
+        def _():
+            arrived(c, 1, slot)
+
+        if k == nx - 1:
+            out_ref[d] = own[c]
             return
-        zsend[c] = total.astype(zsend.dtype)
+        right = target > gx
+        side = jnp.where(right, 0, 1)
+        zsend[c] = own[c].astype(zsend.dtype)
         copy = pltpu.make_async_remote_copy(
-            src_ref=zsend.at[c], dst_ref=zrecv.at[c],
-            send_sem=zs_sem.at[c], recv_sem=zr_sem.at[c],
-            device_id={"gx": lax.rem(gx + offsets[k], nx)}, device_id_type=MESH,
+            src_ref=zsend.at[c], dst_ref=zrecv.at[side, slot],
+            send_sem=zs_sem.at[c], recv_sem=zr_sem.at[side, slot],
+            device_id={"gx": jnp.where(right, gx + 1, gx - 1)}, device_id_type=MESH,
         )
         copy.start()
         z_copies[c] = copy
@@ -297,13 +325,8 @@
         pass_on(k, 0)
     for k in range(nx):
         pass_on(k, 1)
-    last = 2 * (nx - 1)
-    for d in range(2):
-        total = own[last + d]
-        for k in range(nx - 1):
-            z_copies[2 * k + d].wait()
-            total = total + zrecv[2 * k + d].astype(f32)
-        out_ref[d] = total
+    for c in z_copies:
+        z_copies[c].wait_send()
 
 
 def fused(eigen_modes, links_first, links_second):
@@ -354,14 +377,14 @@
             pltpu.VMEM((count,) + chunk, bf16),
             pltpu.VMEM((count,) + chunk, bf16),
             pltpu.VMEM((count - 2,) + chunk, bf16),
-            pltpu.VMEM((count - 2,) + chunk, bf16),
+            pltpu.VMEM((2, count) + chunk, bf16),
             pltpu.SemaphoreType.DMA((3,)),
             pltpu.SemaphoreType.DMA((9,)),
             pltpu.SemaphoreType.DMA((9,)),
             pltpu.SemaphoreType.DMA((count,)),
             pltpu.SemaphoreType.DMA((count,)),
             pltpu.SemaphoreType.DMA((count - 2,)),
-            pltpu.SemaphoreType.DMA((count - 2,)),
+            pltpu.SemaphoreType.DMA((2, count)),
         ],
         compiler_params=pltpu.CompilerParams(
             collective_id=0, has_side_effects=True, vmem_limit_bytes=24 * 1024 * 1024

time: 30.7 us -> 39.4 us (1.28)
  Pallas kernels: 29.9 us -> 38.6 us
    pallas_call x1, Pallas kernels: 29.9 us -> 38.6 us  [fused(): pl.pallas_call(functools.partial(fused_kernel, nx), out_shape=jax.ShapeDt...]
where the time goes in v6:
time: 39.4 us; the launch traced here: 39.3 us
  Pallas kernels  38.6 us (98%)
  local copies, waits for them, and re-layouts  0.71 us (2%)
    pallas_call x1, Pallas kernels, fused(): pl.pallas_call(functools.partial(fused_kernel, nx), out_shape=jax.ShapeDt...  38.6 us

profile of v6, /device:TPU:0, one launch (start us, length us, event | category | flops | bytes accessed | tf_op | source)
XLA Modules:
  0.0 39.3 jit_solution(12523986342010364130)
XLA Ops:
  0.0 38.6 %shard_map.37 = f32[2,2,64,256]{3,2,1,0:T(8,128)S(1)} custom-call(bf16[2,8,16,3,2,256]{5,4,3,2,1,0:T(2,128)(2,1)} %bitcast.7, bf16[18,8,2,16]{3,2,1,0:T(2,128)(2,1)} %bitcast.8, bf16[18,8,2,16]{3,2,1,0:T(2,128)(2,1)} %bitcast.9), custom_call_target="tpu_custom_call" | custom-call | tf_op jit(solution)/shard_map/pallas_call | solution.py:349
  38.6 0.7 %copy.5 = f32[2,2,64,256]{3,2,1,0:T(8,128)} copy(f32[2,2,64,256]{3,2,1,0:T(8,128)S(1)} %shard_map.37) | data formatting | bytes 524288

commit v7 on v5

--- a/solution.py
+++ b/solution.py
@@ -122,10 +122,6 @@
                 vs[p, c, x] = v_ref[p, x, :, c].reshape(sites, width)
         return carry
 
-    for copy in staged:
-        copy.wait()
-    lax.fori_loop(0, planes, relay, 0)
-    pl.semaphore_wait(barrier, nx + 1)
 
     def send(i, src, dst, target):
         copy = pltpu.make_async_remote_copy(
@@ -135,9 +131,14 @@
         copy.start()
         return copy
 
+    staged[0].wait()
+    pl.semaphore_wait(barrier, nx + 1)
     copy_up = send(1, v_ref.at[:, planes - 1], hloraw, {"gx": up})
+    copy_down = send(0, v_ref.at[:, 0], hupraw, {"gx": down})
+    for copy in staged[1:]:
+        copy.wait()
+    lax.fori_loop(0, planes, relay, 0)
     copy_cx = send(2, cf.at[planes - 1], chx, {"gx": up})
-    copy_down = send(0, v_ref.at[:, 0], hupraw, {"gx": down})
     copy_cy = send(3, ce, chy, {"gy": other})
     span = planes * sites
     for p in range(2):

time: 30.7 us -> 29.8 us (0.971)
  Pallas kernels: 29.9 us -> 28.9 us
    pallas_call x1, Pallas kernels: 29.9 us -> 28.9 us  [fused(): pl.pallas_call(functools.partial(fused_kernel, nx), out_shape=jax.ShapeDt...]
where the time goes in v7:
time: 29.8 us; the launch traced here: 29.6 us
  Pallas kernels  28.9 us (97%)
  local copies, waits for them, and re-layouts  0.71 us (2%)
    pallas_call x1, Pallas kernels, fused(): pl.pallas_call(functools.partial(fused_kernel, nx), out_shape=jax.ShapeDt...  28.9 us
    unnamed x1, local copies, waits for them, and re-layouts  0.71 us

profile of v7, /device:TPU:0, one launch (start us, length us, event | category | flops | bytes accessed | tf_op | source)
XLA Modules:
  0.0 29.6 jit_solution(18344657354351619357)
XLA Ops:
  0.0 28.9 %shard_map.37 = f32[2,2,64,256]{3,2,1,0:T(8,128)S(1)} custom-call(bf16[2,8,16,3,2,256]{5,4,3,2,1,0:T(2,128)(2,1)} %bitcast.7, bf16[18,8,2,16]{3,2,1,0:T(2,128)(2,1)} %bitcast.8, bf16[18,8,2,16]{3,2,1,0:T(2,128)(2,1)} %bitcast.9), custom_call_target="tpu_custom_call" | custom-call | tf_op jit(solution)/shard_map/pallas_call | solution.py:327
  28.9 0.7 %copy.5 = f32[2,2,64,256]{3,2,1,0:T(8,128)} copy(f32[2,2,64,256]{3,2,1,0:T(8,128)S(1)} %shard_map.37) | data formatting | bytes 524288
